TPU v7x, 256 devices: a whole 4x4x8 slice. The times are simulated.
256 devices in a mesh: seq: 64 (over z, y, core), head: 4 (over x).
Axes of the slice: x: 4, y: 4, z: 8, core: 2. Of those that a mesh axis runs over, the one named last changes fastest.
Arguments:
- queries: bfloat16 [16384, 4096], P('seq', 'head'), may hold values from -80 to 80, as said below
- keys_in: bfloat16 [16384, 4096], P('seq', 'head'), may hold values from -4 to 4
- values_in: bfloat16 [16384, 4096], P('seq', 'head'), may hold values from -6 to 6
- out_weight: bfloat16 [4096, 4096], P('head'), may hold values from -0.09375 to 0.09375
- spans: int32 [32], P('head'), may hold values from 1024 to 4096
- full_ids: int32 [8], P('head'), may hold values from 0 to 31, as said below
Outputs:
- mixed: bfloat16 [16384, 4096], P('seq', 'head')
Inputs may be any that keep to these rules, and one draw needn't show every extreme that they name: `queries`: unlike a plain normal draw, some rows may be far larger than the rest. `full_ids`: increasing and distinct; entries g * 2 to (g + 1) * 2 - 1 name heads of group g, that is heads g * 8 to (g + 1) * 8 - 1.
All inputs are finite; a program needn't handle non-finite values.
Results may differ from a plain program's by a relative error of at most 0.012.
Values may be sent and summed in bfloat16 or wider, within the bound.
A program may use at most 128 MiB of HBM per device.

v0:
```python
import math

import jax
import jax.numpy as jnp
from jax import lax
from jax.sharding import PartitionSpec as P

HEAD_DIM = 128
SPAN_MAX = 4096


NEG_FILL = -1e30


def from_behind(block, axis, distance):
    devices = range(lax.axis_size(axis))
    route = [(i - distance, i) for i in devices if i - distance in devices]
    return lax.ppermute(block, axis, route)


def split_up(x, dim, devices):
    shape = x.shape
    blocks = x.reshape(*shape[:dim], devices, shape[dim] // devices, *shape[dim + 1 :])
    return jnp.moveaxis(blocks, dim, 0)


def sum_at_owner(x, axis, dim):
    devices = lax.axis_size(axis)
    blocks = lax.all_to_all(split_up(x, dim, devices), axis, 0, 0, tiled=True)
    return jnp.sum(blocks.astype(jnp.float32), axis=0)


def online_update(carry_state, scores, allowed, value_rows):
    old_peak, row_total, numerator = carry_state
    masked = jnp.where(allowed, scores, NEG_FILL)
    new_peak = jnp.maximum(old_peak, jnp.max(masked, axis=-1))
    weights = jnp.where(allowed, jnp.exp(masked - new_peak[..., None]), 0.0)
    rescale = jnp.exp(old_peak - new_peak)
    row_total = row_total * rescale + jnp.sum(weights, axis=-1)
    numerator = numerator * rescale[..., None] + jnp.einsum(
        "hqk,hkd->hqd", weights.astype(jnp.bfloat16), value_rows, preferred_element_type=jnp.float32
    )
    return (new_peak, row_total, numerator)


def empty_state(lead_count, row_count, head_width):
    return (
        jnp.full((lead_count, row_count), NEG_FILL, jnp.float32),
        jnp.zeros((lead_count, row_count), jnp.float32),
        jnp.zeros((lead_count, row_count, head_width), jnp.float32),
    )


def finish(carry_state):
    return (carry_state[2] / carry_state[1][..., None]).astype(jnp.bfloat16)


def causal_piece(query_rows, first_row, key_rows, value_rows, score_scale):
    row_count = query_rows.shape[1]
    tile_rows = math.gcd(2048, key_rows.shape[1])
    query_pos = first_row + jnp.arange(row_count)
    tile_count = (first_row + row_count + tile_rows - 1) // tile_rows

    def absorb_tile(tile_index, inner_state):
        key_tile = lax.dynamic_slice_in_dim(key_rows, tile_index * tile_rows, tile_rows, 1)
        value_tile = lax.dynamic_slice_in_dim(value_rows, tile_index * tile_rows, tile_rows, 1)
        key_pos = tile_index * tile_rows + jnp.arange(tile_rows)
        scores = (
            jnp.einsum("hqd,hkd->hqk", query_rows, key_tile, preferred_element_type=jnp.float32)
            * score_scale
        )
        allowed = key_pos[None, None, :] <= query_pos[None, :, None]
        return online_update(inner_state, scores, allowed, value_tile)

    return lax.fori_loop(0, tile_count, absorb_tile, empty_state(1, row_count, query_rows.shape[2]))


def on_device(queries, keys_in, values_in, out_weight, spans, full_ids):
    score_scale = HEAD_DIM ** (-0.5)
    n_seq = lax.axis_size("seq")
    seq_index = lax.axis_index("seq")
    tok_rows = queries.shape[0]
    group_heads = queries.shape[1] // HEAD_DIM
    full_count = full_ids.shape[0]
    band_count = group_heads - full_count
    head_base = lax.axis_index("head") * group_heads
    local_range = jnp.arange(group_heads)
    marks = jnp.sum(
        (local_range[:, None] + head_base == full_ids[None, :]).astype(jnp.int32), axis=1
    )
    order_local = jnp.argsort(marks * group_heads + local_range)
    band_local = order_local[:band_count]
    full_local = order_local[band_count:]
    query_three = queries.reshape(tok_rows, group_heads, HEAD_DIM)
    key_three = keys_in.reshape(tok_rows, group_heads, HEAD_DIM)
    value_three = values_in.reshape(tok_rows, group_heads, HEAD_DIM)
    query_band = jnp.take(query_three, band_local, axis=1).transpose(1, 0, 2)
    kv_band = jnp.stack(
        [
            jnp.take(key_three, band_local, axis=1).transpose(1, 0, 2),
            jnp.take(value_three, band_local, axis=1).transpose(1, 0, 2),
        ]
    )
    band_reach = jnp.take(spans, band_local)
    query_pos = seq_index * tok_rows + jnp.arange(tok_rows)
    hop_count = min(max(1, SPAN_MAX // tok_rows), n_seq - 1)
    arrived = [(kv_band, 0)]
    moving = kv_band
    for distance in range(1, hop_count + 1):
        moving = from_behind(moving, "seq", 1)
        arrived.append((moving, distance))
    batch_size = max(1, 512 // tok_rows)
    band_state = empty_state(band_count, tok_rows, HEAD_DIM)
    for first_piece in range(0, len(arrived), batch_size):
        batch_pieces = arrived[first_piece : first_piece + batch_size]
        key_rows = jnp.concatenate([arrival[0][0] for arrival in batch_pieces], axis=1)
        value_rows = jnp.concatenate([arrival[0][1] for arrival in batch_pieces], axis=1)
        key_pos = jnp.concatenate(
            [(seq_index - arrival[1]) * tok_rows + jnp.arange(tok_rows) for arrival in batch_pieces]
        )
        scores = (
            jnp.einsum("hqd,hkd->hqk", query_band, key_rows, preferred_element_type=jnp.float32)
            * score_scale
        )
        gap_size = query_pos[None, :, None] - key_pos[None, None, :]
        allowed = (
            (gap_size >= 0) & (gap_size < band_reach[:, None, None]) & (key_pos >= 0)[None, None, :]
        )
        band_state = online_update(band_state, scores, allowed, value_rows)
    band_out = finish(band_state)
    query_full = jnp.take(query_three, full_local, axis=1).transpose(1, 0, 2)
    key_full = jnp.take(key_three, full_local, axis=1).transpose(1, 0, 2)
    value_full = jnp.take(value_three, full_local, axis=1).transpose(1, 0, 2)
    block_count = n_seq // full_count
    halfway = full_count // 2
    slab = seq_index // halfway
    own_block = jnp.where(slab < block_count, slab, 2 * block_count - 1 - slab)
    slot_block = jnp.arange(n_seq) % block_count

    def spread(array):
        return jnp.broadcast_to(
            array[:, None], (full_count, block_count, tok_rows, HEAD_DIM)
        ).reshape(n_seq, tok_rows, HEAD_DIM)

    keep_rows = (slot_block == own_block)[:, None, None]
    query_send = jnp.where(keep_rows, spread(query_full), jnp.zeros((), jnp.bfloat16))
    query_recv, key_recv, value_recv = (
        lax.all_to_all(query_send, "seq", split_axis=0, concat_axis=0, tiled=True),
        lax.all_to_all(spread(key_full), "seq", split_axis=0, concat_axis=0, tiled=True),
        lax.all_to_all(spread(value_full), "seq", split_axis=0, concat_axis=0, tiled=True),
    )
    dest_block = seq_index % block_count
    query_sources = [
        (dest_block * halfway, halfway),
        ((2 * block_count - 1 - dest_block) * halfway, halfway),
    ]
    key_rows = key_recv.reshape(1, n_seq * tok_rows, HEAD_DIM)
    value_rows = value_recv.reshape(1, n_seq * tok_rows, HEAD_DIM)
    send_back = jnp.zeros((n_seq, tok_rows, HEAD_DIM), jnp.bfloat16)
    for source_first, source_count in query_sources:
        query_rows = lax.dynamic_slice_in_dim(query_recv, source_first, source_count, 0)
        piece_state = causal_piece(
            query_rows, source_first * tok_rows, key_rows, value_rows, score_scale
        )
        piece_out = finish(piece_state)
        send_back = lax.dynamic_update_slice_in_dim(send_back, piece_out, source_first, 0)
    returned = lax.all_to_all(send_back, "seq", split_axis=0, concat_axis=0, tiled=True)
    full_out = lax.dynamic_index_in_dim(
        returned.reshape(full_count, block_count, tok_rows, HEAD_DIM), own_block, 1, keepdims=False
    )
    combined = jnp.concatenate([band_out, full_out], axis=0)
    inverse = jnp.argsort(order_local)
    per_head = jnp.take(combined, inverse, axis=0)
    attended = per_head.transpose(1, 0, 2).reshape(tok_rows, group_heads * HEAD_DIM)
    projected = jnp.dot(attended, out_weight, preferred_element_type=jnp.float32)
    return sum_at_owner(projected.astype(jnp.bfloat16), "head", 1).astype(jnp.bfloat16)


def solution(mesh):
    placed = (
        P("seq", "head"),
        P("seq", "head"),
        P("seq", "head"),
        P("head", None),
        P("head"),
        P("head"),
    )
    return jax.shard_map(
        on_device, mesh=mesh, in_specs=placed, out_specs=P("seq", "head"), check_vma=False
    )
```

profile of v0, /device:TPU:25, one launch (start us, length us, event | category | flops | bytes accessed | tf_op | source)
XLA Modules:
  0.0 729.2 jit_solution(2009998074109659581)
XLA Ops:
  10.4 12.4 %all-to-all-start = ((bf16[64,256,128]{2,1,0:T(8,128)(2,1)}), bf16[64,256,128]{2,1,0:T(8,128)(2,1)}, u32[]{:S(2)}, u32[]{:S(2)}) async-start(bf16[64,256,128]{2,1,0:T(8,128)(2,1)} %bitcast.199), calls=%async_computation | async-start | bytes 8388608 | tf_op jit(solution)/shard_map/all_to_all | solution.py:149
  25.1 91.3 %all-to-all-done = bf16[64,256,128]{2,1,0:T(8,128)(2,1)} async-done(((bf16[64,256,128]{2,1,0:T(8,128)(2,1)}), bf16[64,256,128]{2,1,0:T(8,128)(2,1)}, u32[]{:S(2)}, u32[]{:S(2)}) %all-to-all-start) | async-done | bytes 4194336 | tf_op jit(solution)/shard_map/all_to_all | solution.py:149
  116.5 8.1 %all-to-all-start.1 = ((bf16[64,256,128]{2,1,0:T(8,128)(2,1)}), bf16[64,256,128]{2,1,0:T(8,128)(2,1)}, u32[]{:S(2)}, u32[]{:S(2)}) async-start(bf16[64,256,128]{2,1,0:T(8,128)(2,1)} %bitcast_select_fusion), calls=%async_computation.1 | async-start | bytes 8388608 | tf_op jit(solution)/shard_map/all_to_all | solution.py:148
  131.5 91.7 %collective-permute-done = bf16[2,6,256,128]{3,2,1,0:T(8,128)(2,1)S(1)} collective-permute-done((bf16[2,6,256,128]{3,2,1,0:T(8,128)(2,1)}, bf16[2,6,256,128]{3,2,1,0:T(8,128)(2,1)S(1)}, u32[]{:S(2)}, u32[]{:S(2)}) %collective-permute-start) | collective-permute-done | bytes 786464 | tf_op jit(solution)/shard_map/ppermute | solution.py:18
  223.1 6.4 collective-permute-start.1
  230.7 7.8 %collective-permute-done.1 = bf16[2,6,256,128]{3,2,1,0:T(8,128)(2,1)} collective-permute-done((bf16[2,6,256,128]{3,2,1,0:T(8,128)(2,1)S(1)}, bf16[2,6,256,128]{3,2,1,0:T(8,128)(2,1)}, u32[]{:S(2)}, u32[]{:S(2)}) %collective-permute-start.1) | collective-permute-done | bytes 786464 | tf_op jit(solution)/shard_map/ppermute | solution.py:18
  238.5 6.6 collective-permute-start.2
  248.6 10.3 %all-to-all-start.2 = ((bf16[64,256,128]{2,1,0:T(8,128)(2,1)}), bf16[64,256,128]{2,1,0:T(8,128)(2,1)}, u32[]{:S(2)}, u32[]{:S(2)}) async-start(bf16[64,256,128]{2,1,0:T(8,128)(2,1)} %bitcast.198), calls=%async_computation.2 | async-start | bytes 8388608 | tf_op jit(solution)/shard_map/all_to_all | solution.py:150
  265.1 92.4 %collective-permute-done.3 = bf16[2,6,256,128]{3,2,1,0:T(8,128)(2,1)S(1)} collective-permute-done((bf16[2,6,256,128]{3,2,1,0:T(8,128)(2,1)}, bf16[2,6,256,128]{3,2,1,0:T(8,128)(2,1)S(1)}, u32[]{:S(2)}, u32[]{:S(2)}) %collective-permute-start.3) | collective-permute-done | bytes 786464 | tf_op jit(solution)/shard_map/ppermute | solution.py:18
  357.4 6.4 collective-permute-start.4
  368.0 4.7 collective-permute-done.4
  372.7 6.6 collective-permute-start.5
  382.3 6.2 collective-permute-done.5
  388.6 6.4 collective-permute-start.6
  403.9 6.5 collective-permute-start.7
  413.7 5.6 collective-permute-done.7
  419.3 6.5 collective-permute-start.8
  428.0 6.6 collective-permute-done.8
  434.7 6.7 collective-permute-start.9
  441.6 5.1 fusion.46
  450.1 6.6 collective-permute-start.10
  461.5 4.9 while.30
  466.4 6.8 collective-permute-start.11
  474.5 39.3 %while.31 = (s32[]{:T(128)}, f32[1,256]{1,0:T(1,128)S(1)}, f32[1,256]{1,0:T(1,128)}, f32[1,256,128]{2,1,0:T(8,128)}, s32[]{:T(128)}, /*index=5*/bf16[1,16384,128...) while((s32[]{:T(128)}, f32[1,256]{1,0:T(1,128)S(1)}, ...), condition=%wide.region_28.31_spmd.clone, body=%wide.region_25.30_spmd.clone.sunk | while | flops 274795264 | bytes 8778035 | solution.py:75
  520.3 16.8 %all-to-all-start.3 = ((bf16[64,256,128]{2,1,0:T(8,128)(2,1)}), bf16[64,256,128]{2,1,0:T(8,128)(2,1)}, u32[]{:S(2)}, u32[]{:S(2)}) async-start(bf16[64,256,128]{2,1,0:T(8,128)(2,1)} %fusion.218), calls=%async_computation.3 | async-start | bytes 8388608 | tf_op jit(solution)/shard_map/all_to_all | solution.py:167
  546.7 89.0 %collective-permute-done.13 = bf16[2,6,256,128]{3,2,1,0:T(8,128)(2,1)S(1)} collective-permute-done((bf16[2,6,256,128]{3,2,1,0:T(8,128)(2,1)}, bf16[2,6,256,128]{3,2,1,0:T(8,128)(2,1)S(1)}, u32[]{:S(2)}, u32[]{:S(2)}) %collective-permute-start.13) | collective-permute-done | bytes 786464 | tf_op jit(solution)/shard_map/ppermute | solution.py:18
  635.7 16.2 %collective-permute-start.14 = (bf16[2,6,256,128]{3,2,1,0:T(8,128)(2,1)S(1)}, bf16[2,6,256,128]{3,2,1,0:T(8,128)(2,1)S(1)}, u32[]{:S(2)}, u32[]{:S(2)}) collective-permute-start(bf16[2,6,256,128]{3,2,1,0:T(8,128)(2,1)S(1)} %collective-permute-done.13), channel_id=1, source_target_pairs={{0,4},{4,8},{8,12},{12,16},{16,20},{20,24},{24,28},{28,32},{32,36}... | collective-permute-start | bytes 2359304 | tf_op jit(solution)/shard_map/ppermute | solution.py:18
  652.1 4.5 fusion.48
  663.2 4.6 collective-permute-done.15
  670.7 4.8 fusion.54
  691.9 5.8 convolution_convert_fusion
  697.8 29.6 %all_to_all.25 = bf16[4,256,1024]{2,1,0:T(8,128)(2,1)S(1)} all-to-all(bf16[4,256,1024]{2,1,0:T(8,128)(2,1)S(1)} %bitcast.201), channel_id=1, replica_groups=mesh['seq'=64,'head'=4] {'head'}, dimensions={0} | all-to-all | bytes 4194304 | tf_op jit(solution)/shard_map/all_to_all | solution.py:29
  (437 shorter events, 147.4 us)
Async XLA Ops:
  0.0 262.8 %copy-start = (s32[8]{0:T(128)S(1)}, s32[8]{0:T(128)}, u32[]{:S(2)}) copy-start(s32[8]{0:T(128)} %param.18) | copy-start | bytes 100
  10.4 106.1 %all-to-all-start = ((bf16[64,256,128]{2,1,0:T(8,128)(2,1)}), bf16[64,256,128]{2,1,0:T(8,128)(2,1)}, u32[]{:S(2)}, u32[]{:S(2)}) async-start(bf16[64,256,128]{2,1,0:T(8,128)(2,1)} %bitcast.199), calls=%async_computation | async-start | bytes 8388608 | tf_op jit(solution)/shard_map/all_to_all | solution.py:149
  116.5 129.1 %all-to-all-start.1 = ((bf16[64,256,128]{2,1,0:T(8,128)(2,1)}), bf16[64,256,128]{2,1,0:T(8,128)(2,1)}, u32[]{:S(2)}, u32[]{:S(2)}) async-start(bf16[64,256,128]{2,1,0:T(8,128)(2,1)} %bitcast_select_fusion), calls=%async_computation.1 | async-start | bytes 8388608 | tf_op jit(solution)/shard_map/all_to_all | solution.py:148
  124.6 316.9 %copy-start.60 = (pred[6]{0:T(512)(128)(4,1)}, pred[6]{0:T(512)(128)(4,1)S(1)}, u32[]{:S(2)}) copy-start(pred[6]{0:T(512)(128)(4,1)S(1)} %get-tuple-element.228) | copy-start | bytes 22
  126.0 122.5 %copy-start.8 = (bf16[6,256,128]{2,1,0:T(8,128)(2,1)}, bf16[6,256,128]{2,1,0:T(8,128)(2,1)S(1)}, u32[]{:S(2)}) copy-start(bf16[6,256,128]{2,1,0:T(8,128)(2,1)S(1)} %get-tuple-element.286) | copy-start | bytes 1179652
  127.1 96.1 %collective-permute-start = (bf16[2,6,256,128]{3,2,1,0:T(8,128)(2,1)}, bf16[2,6,256,128]{3,2,1,0:T(8,128)(2,1)S(1)}, u32[]{:S(2)}, u32[]{:S(2)}) collective-permute-start(bf16[2,6,256,128]{3,2,1,0:T(8,128)(2,1)} %pad_maximum_fusion), channel_id=1, source_target_pairs={{0,4},{4,8},{8,12},{12,16},{16,20},{20,24},{24,28},{28,32},{32,36}... | collective-permute-start | bytes 2359304 | tf_op jit(solution)/shard_map/ppermute | solution.py:18
  223.1 15.3 %collective-permute-start.1 = (bf16[2,6,256,128]{3,2,1,0:T(8,128)(2,1)S(1)}, bf16[2,6,256,128]{3,2,1,0:T(8,128)(2,1)}, u32[]{:S(2)}, u32[]{:S(2)}) collective-permute-start(bf16[2,6,256,128]{3,2,1,0:T(8,128)(2,1)S(1)} %collective-permute-done), channel_id=1, source_target_pairs={{0,4},{4,8},{8,12},{12,16},{16,20},{20,24},{24,28},{28,32},{32,36}... | collective-permute-start | bytes 2359304 | tf_op jit(solution)/shard_map/ppermute | solution.py:18
  238.5 21.0 %collective-permute-start.2 = (bf16[2,6,256,128]{3,2,1,0:T(8,128)(2,1)}, bf16[2,6,256,128]{3,2,1,0:T(8,128)(2,1)}, u32[]{:S(2)}, u32[]{:S(2)}) collective-permute-start(bf16[2,6,256,128]{3,2,1,0:T(8,128)(2,1)} %collective-permute-done.1), channel_id=1, source_target_pairs={{0,4},{4,8},{8,12},{12,16},{16,20},{20,24},{24,28},{28,32},{32,36}... | collective-permute-start | bytes 2359304 | tf_op jit(solution)/shard_map/ppermute | solution.py:18
  248.6 211.7 %all-to-all-start.2 = ((bf16[64,256,128]{2,1,0:T(8,128)(2,1)}), bf16[64,256,128]{2,1,0:T(8,128)(2,1)}, u32[]{:S(2)}, u32[]{:S(2)}) async-start(bf16[64,256,128]{2,1,0:T(8,128)(2,1)} %bitcast.198), calls=%async_computation.2 | async-start | bytes 8388608 | tf_op jit(solution)/shard_map/all_to_all | solution.py:150
  259.4 98.0 %collective-permute-start.3 = (bf16[2,6,256,128]{3,2,1,0:T(8,128)(2,1)}, bf16[2,6,256,128]{3,2,1,0:T(8,128)(2,1)S(1)}, u32[]{:S(2)}, u32[]{:S(2)}) collective-permute-start(bf16[2,6,256,128]{3,2,1,0:T(8,128)(2,1)} %collective-permute-done.2), channel_id=1, source_target_pairs={{0,4},{4,8},{8,12},{12,16},{16,20},{20,24},{24,28},{28,32},{32,36}... | collective-permute-start | bytes 2359304 | tf_op jit(solution)/shard_map/ppermute | solution.py:18
  262.8 132.2 %copy-start.81 = (pred[512]{0:T(512)(128)(4,1)}, pred[512]{0:T(512)(128)(4,1)S(1)}, u32[]{:S(2)}) copy-start(pred[512]{0:T(512)(128)(4,1)S(1)} %broadcast_compare_fusion.16) | copy-start | bytes 1540
  265.1 129.9 %copy-start.66 = (s32[6]{0:T(128)}, s32[6]{0:T(128)S(1)}, u32[]{:S(2)}) copy-start(s32[6]{0:T(128)S(1)} %broadcast_select_fusion.6) | copy-start | bytes 76
  357.4 15.3 %collective-permute-start.4 = (bf16[2,6,256,128]{3,2,1,0:T(8,128)(2,1)S(1)}, bf16[2,6,256,128]{3,2,1,0:T(8,128)(2,1)}, u32[]{:S(2)}, u32[]{:S(2)}) collective-permute-start(bf16[2,6,256,128]{3,2,1,0:T(8,128)(2,1)S(1)} %collective-permute-done.3), channel_id=1, source_target_pairs={{0,4},{4,8},{8,12},{12,16},{16,20},{20,24},{24,28},{28,32},{32,36}... | collective-permute-start | bytes 2359304 | tf_op jit(solution)/shard_map/ppermute | solution.py:18
  372.7 15.8 %collective-permute-start.5 = (bf16[2,6,256,128]{3,2,1,0:T(8,128)(2,1)}, bf16[2,6,256,128]{3,2,1,0:T(8,128)(2,1)S(1)}, u32[]{:S(2)}, u32[]{:S(2)}) collective-permute-start(bf16[2,6,256,128]{3,2,1,0:T(8,128)(2,1)} %collective-permute-done.4), channel_id=1, source_target_pairs={{0,4},{4,8},{8,12},{12,16},{16,20},{20,24},{24,28},{28,32},{32,36}... | collective-permute-start | bytes 2359304 | tf_op jit(solution)/shard_map/ppermute | solution.py:18
  388.6 15.3 %collective-permute-start.6 = (bf16[2,6,256,128]{3,2,1,0:T(8,128)(2,1)S(1)}, bf16[2,6,256,128]{3,2,1,0:T(8,128)(2,1)S(1)}, u32[]{:S(2)}, u32[]{:S(2)}) collective-permute-start(bf16[2,6,256,128]{3,2,1,0:T(8,128)(2,1)S(1)} %collective-permute-done.5), channel_id=1, source_target_pairs={{0,4},{4,8},{8,12},{12,16},{16,20},{20,24},{24,28},{28,32},{32,36}... | collective-permute-start | bytes 2359304 | tf_op jit(solution)/shard_map/ppermute | solution.py:18
  403.9 15.4 %collective-permute-start.7 = (bf16[2,6,256,128]{3,2,1,0:T(8,128)(2,1)S(1)}, bf16[2,6,256,128]{3,2,1,0:T(8,128)(2,1)S(1)}, u32[]{:S(2)}, u32[]{:S(2)}) collective-permute-start(bf16[2,6,256,128]{3,2,1,0:T(8,128)(2,1)S(1)} %collective-permute-done.6), channel_id=1, source_target_pairs={{0,4},{4,8},{8,12},{12,16},{16,20},{20,24},{24,28},{28,32},{32,36}... | collective-permute-start | bytes 2359304 | tf_op jit(solution)/shard_map/ppermute | solution.py:18
  419.3 15.4 %collective-permute-start.8 = (bf16[2,6,256,128]{3,2,1,0:T(8,128)(2,1)S(1)}, bf16[2,6,256,128]{3,2,1,0:T(8,128)(2,1)S(1)}, u32[]{:S(2)}, u32[]{:S(2)}) collective-permute-start(bf16[2,6,256,128]{3,2,1,0:T(8,128)(2,1)S(1)} %collective-permute-done.7), channel_id=1, source_target_pairs={{0,4},{4,8},{8,12},{12,16},{16,20},{20,24},{24,28},{28,32},{32,36}... | collective-permute-start | bytes 2359304 | tf_op jit(solution)/shard_map/ppermute | solution.py:18
  434.7 15.4 %collective-permute-start.9 = (bf16[2,6,256,128]{3,2,1,0:T(8,128)(2,1)S(1)}, bf16[2,6,256,128]{3,2,1,0:T(8,128)(2,1)}, u32[]{:S(2)}, u32[]{:S(2)}) collective-permute-start(bf16[2,6,256,128]{3,2,1,0:T(8,128)(2,1)S(1)} %collective-permute-done.8), channel_id=1, source_target_pairs={{0,4},{4,8},{8,12},{12,16},{16,20},{20,24},{24,28},{28,32},{32,36}... | collective-permute-start | bytes 2359304 | tf_op jit(solution)/shard_map/ppermute | solution.py:18
  450.1 16.4 %collective-permute-start.10 = (bf16[2,6,256,128]{3,2,1,0:T(8,128)(2,1)}, bf16[2,6,256,128]{3,2,1,0:T(8,128)(2,1)}, u32[]{:S(2)}, u32[]{:S(2)}) collective-permute-start(bf16[2,6,256,128]{3,2,1,0:T(8,128)(2,1)} %collective-permute-done.9), channel_id=1, source_target_pairs={{0,4},{4,8},{8,12},{12,16},{16,20},{20,24},{24,28},{28,32},{32,36}... | collective-permute-start | bytes 2359304 | tf_op jit(solution)/shard_map/ppermute | solution.py:18
  466.4 51.2 %collective-permute-start.11 = (bf16[2,6,256,128]{3,2,1,0:T(8,128)(2,1)}, bf16[2,6,256,128]{3,2,1,0:T(8,128)(2,1)}, u32[]{:S(2)}, u32[]{:S(2)}) collective-permute-start(bf16[2,6,256,128]{3,2,1,0:T(8,128)(2,1)} %collective-permute-done.10), channel_id=1, source_target_pairs={{0,4},{4,8},{8,12},{12,16},{16,20},{20,24},{24,28},{28,32},{32,36}... | collective-permute-start | bytes 2359304 | tf_op jit(solution)/shard_map/ppermute | solution.py:18
  517.6 22.3 %collective-permute-start.12 = (bf16[2,6,256,128]{3,2,1,0:T(8,128)(2,1)}, bf16[2,6,256,128]{3,2,1,0:T(8,128)(2,1)}, u32[]{:S(2)}, u32[]{:S(2)}) collective-permute-start(bf16[2,6,256,128]{3,2,1,0:T(8,128)(2,1)} %collective-permute-done.11), channel_id=1, source_target_pairs={{0,4},{4,8},{8,12},{12,16},{16,20},{20,24},{24,28},{28,32},{32,36}... | collective-permute-start | bytes 2359304 | tf_op jit(solution)/shard_map/ppermute | solution.py:18
  520.3 169.4 %all-to-all-start.3 = ((bf16[64,256,128]{2,1,0:T(8,128)(2,1)}), bf16[64,256,128]{2,1,0:T(8,128)(2,1)}, u32[]{:S(2)}, u32[]{:S(2)}) async-start(bf16[64,256,128]{2,1,0:T(8,128)(2,1)} %fusion.218), calls=%async_computation.3 | async-start | bytes 8388608 | tf_op jit(solution)/shard_map/all_to_all | solution.py:167
  539.9 95.8 %collective-permute-start.13 = (bf16[2,6,256,128]{3,2,1,0:T(8,128)(2,1)}, bf16[2,6,256,128]{3,2,1,0:T(8,128)(2,1)S(1)}, u32[]{:S(2)}, u32[]{:S(2)}) collective-permute-start(bf16[2,6,256,128]{3,2,1,0:T(8,128)(2,1)} %collective-permute-done.12), channel_id=1, source_target_pairs={{0,4},{4,8},{8,12},{12,16},{16,20},{20,24},{24,28},{28,32},{32,36}... | collective-permute-start | bytes 2359304 | tf_op jit(solution)/shard_map/ppermute | solution.py:18
  543.3 108.6 %copy-start.86 = (f32[6,256,512]{2,1,0:T(8,128)S(1)}, f32[6,256,512]{2,1,0:T(8,128)}, u32[]{:S(2)}) copy-start(f32[6,256,512]{2,1,0:T(8,128)} %get-tuple-element.294) | copy-start | bytes 9437188
  544.6 107.3 %copy-start.4 = (s32[256,512]{1,0:T(8,128)S(1)}, s32[256,512]{1,0:T(8,128)}, u32[]{:S(2)}) copy-start(s32[256,512]{1,0:T(8,128)} %get-tuple-element.277) | copy-start | bytes 1572868
  544.6 107.3 %copy-start.5 = (s32[256,512]{1,0:T(8,128)S(1)}, s32[256,512]{1,0:T(8,128)}, u32[]{:S(2)}) copy-start(s32[256,512]{1,0:T(8,128)} %get-tuple-element.282) | copy-start | bytes 1572868
  544.6 107.3 %copy-start.6 = (s32[256,512]{1,0:T(8,128)S(1)}, s32[256,512]{1,0:T(8,128)}, u32[]{:S(2)}) copy-start(s32[256,512]{1,0:T(8,128)} %get-tuple-element.281) | copy-start | bytes 1572868
  544.6 107.3 %copy-start.11 = (pred[256,512]{1,0:T(8,128)(4,1)S(1)}, pred[256,512]{1,0:T(8,128)(4,1)}, u32[]{:S(2)}) copy-start(pred[256,512]{1,0:T(8,128)(4,1)} %get-tuple-element.269) | copy-start | bytes 393220
  544.6 107.3 %copy-start.12 = (pred[256,512]{1,0:T(8,128)(4,1)S(1)}, pred[256,512]{1,0:T(8,128)(4,1)}, u32[]{:S(2)}) copy-start(pred[256,512]{1,0:T(8,128)(4,1)} %get-tuple-element.271) | copy-start | bytes 393220
  544.7 107.3 %copy-start.13 = (pred[256,512]{1,0:T(8,128)(4,1)S(1)}, pred[256,512]{1,0:T(8,128)(4,1)}, u32[]{:S(2)}) copy-start(pred[256,512]{1,0:T(8,128)(4,1)} %get-tuple-element.272) | copy-start | bytes 393220
  635.7 21.0 %collective-permute-start.14 = (bf16[2,6,256,128]{3,2,1,0:T(8,128)(2,1)S(1)}, bf16[2,6,256,128]{3,2,1,0:T(8,128)(2,1)S(1)}, u32[]{:S(2)}, u32[]{:S(2)}) collective-permute-start(bf16[2,6,256,128]{3,2,1,0:T(8,128)(2,1)S(1)} %collective-permute-done.13), channel_id=1, source_target_pairs={{0,4},{4,8},{8,12},{12,16},{16,20},{20,24},{24,28},{28,32},{32,36}... | collective-permute-start | bytes 2359304 | tf_op jit(solution)/shard_map/ppermute | solution.py:18
  656.7 11.1 %collective-permute-start.15 = (bf16[2,6,256,128]{3,2,1,0:T(8,128)(2,1)S(1)}, bf16[2,6,256,128]{3,2,1,0:T(8,128)(2,1)S(1)}, u32[]{:S(2)}, u32[]{:S(2)}) collective-permute-start(bf16[2,6,256,128]{3,2,1,0:T(8,128)(2,1)S(1)} %collective-permute-done.14), channel_id=1, source_target_pairs={{0,4},{4,8},{8,12},{12,16},{16,20},{20,24},{24,28},{28,32},{32,36}... | collective-permute-start | bytes 2359304 | tf_op jit(solution)/shard_map/ppermute | solution.py:18
  (103 other events, 2077.7 us)
where the time goes:
time: 739 us; the launch traced here: 729 us
  waiting for transfers between devices  404 us (55%)
  starting transfers between devices  143 us (19%)
  matrix products  71.5 us (10%)
  local copies, waits for them, and re-layouts  46.7 us (6%)
  other arithmetic  31.2 us (4%)
  blocking collectives  29.6 us (4%)
    ppermute x16, waiting for transfers between devices, from_behind(): return lax.ppermute(block, axis, route)  313 us
    ppermute x16, starting transfers between devices, from_behind(): return lax.ppermute(block, axis, route)  95.7 us
    all_to_all x1, waiting for transfers between devices, on_device(): lax.all_to_all(spread(key_full), 'seq', split_axis=0, concat_axis=0, tile...  91.3 us
    dot_general x18, matrix products, online_update(): jnp.einsum('hqk,hkd->hqd', weights.astype(jnp.bfloat16), value_rows, pref...  31.3 us
    all_to_all x1, blocking collectives, sum_at_owner(): blocks = lax.all_to_all(split_up(x, dim, devices), axis, 0, 0, tiled=True)  29.6 us
    dot_general x9, matrix products, on_device(): jnp.einsum('hqd,hkd->hqk', query_band, key_rows, preferred_element_type=j...  19 us
    squeeze x15, local copies, waits for them, and re-layouts, on_device(): arrival[0][1]  17.6 us
    all_to_all x1, starting transfers between devices, on_device(): lax.all_to_all(send_back, 'seq', split_axis=0, concat_axis=0, tiled=True)  16.8 us
  transfers between devices with their start and end apart: 20, of which 12 were waited for; matrix products, arithmetic and copies ran while one was open for 17% of the time, Pallas kernels for 0%

commit v1 on v0

v1 whole, which is shorter than its diff:
```python
import functools
import math

import jax
import jax.numpy as jnp
from jax import lax
from jax.experimental import pallas as pl
from jax.experimental.pallas import tpu as pltpu
from jax.sharding import PartitionSpec as P

HD = 128
ROWS = 256
SCALE2 = HD ** (-0.5) * math.log2(math.e)
FILL = -1e30
FLOOR = -5e29
MESH = pl.DeviceIdType.MESH
ANY = pl.BlockSpec(memory_space=pl.ANY)
VM = pl.BlockSpec(memory_space=pltpu.VMEM)
BF = jnp.bfloat16
F32 = jnp.float32


def position():
    s = lax.axis_index("seq")
    return s, s // 8, (s // 2) % 4, s % 2, lax.axis_index("head")


def pick(slot, f0, f1):
    h = slot + (slot >= f0).astype(jnp.int32)
    h = h + (h >= f1).astype(jnp.int32)
    return jnp.where(slot == 6, f0, jnp.where(slot == 7, f1, h))


def local_full(full_ref):
    base = lax.axis_index("head") * 8
    return full_ref[0] - base, full_ref[1] - base


def arrange_body(ids, q, k, v, qh, kvh):
    qh[0] = q[...]
    kvh[0, 0] = k[...]
    kvh[0, 1] = v[...]


def arrange(local_ids, q, k, v):
    def column(i, ids):
        return (0, pick(i, ids[0], ids[1]))

    block = pl.BlockSpec((ROWS, HD), column)
    return pl.pallas_call(
        arrange_body,
        out_shape=(
            jax.ShapeDtypeStruct((8, ROWS, HD), BF),
            jax.ShapeDtypeStruct((8, 2, ROWS, HD), BF),
        ),
        grid_spec=pltpu.PrefetchScalarGridSpec(
            num_scalar_prefetch=1,
            grid=(8,),
            in_specs=[block, block, block],
            out_specs=[
                pl.BlockSpec((1, ROWS, HD), lambda i, ids: (i, 0, 0)),
                pl.BlockSpec((1, 2, ROWS, HD), lambda i, ids: (i, 0, 0, 0)),
            ],
        ),
        name="arrange",
    )(local_ids, q, k, v)


def greet(targets):
    barrier = pltpu.get_barrier_semaphore()
    for target in targets:
        pl.semaphore_signal(barrier, inc=1, device_id=target, device_id_type=MESH)
    pl.semaphore_wait(barrier, len(targets))


def plane_peers(s, hd):
    base = (s // 8) * 8
    return [(base + (s + r) % 8, hd) for r in range(1, 8)]


class Push:
    def __init__(self, src, dst, ssem, rsem, target, me, hd):
        self.remote = pltpu.make_async_remote_copy(
            src_ref=src, dst_ref=dst, send_sem=ssem, recv_sem=rsem, device_id=(target, hd), device_id_type=MESH
        )
        self.local = pltpu.make_async_copy(src, dst, rsem)
        self.away = target != me

    def start(self):
        @pl.when(self.away)
        def _():
            self.remote.start()

        @pl.when(jnp.logical_not(self.away))
        def _():
            self.local.start()

    def wait_send(self):
        @pl.when(self.away)
        def _():
            self.remote.wait_send()


def landed(ref, sem):
    pltpu.make_async_copy(ref, ref, sem).wait()


def exchange_body(
    qh, kvh, qb, kva, kvb, kvf, s_in, r_in, s_q, r_q, s_fa, r_fa, s_fb, r_fb, s_ff, r_ff, s_sa, r_sa, s_sb, r_sb, s_sf, r_sf
):
    s, z, y, c, hd = position()
    base = z * 8
    up, down = (s + 8) % 64, (s + 56) % 64
    sib = base + 2 * y + (1 - c)
    greet(plane_peers(s, hd) + [(up, hd), (down, hd)])

    sends = []

    def push(src, dst, ssem, rsem, target):
        one = Push(src, dst, ssem, rsem, target, s, hd)
        one.start()
        sends.append(one)

    half = y // 2
    for g in range(2):
        push(kvh.at[6 + g], kvf.at[z, c_of(y), y % 2], s_in.at[g], r_in.at[y % 2], base + 2 * (2 * g + c) + half)
    for t in range(4):
        push(kvh.at[t], kva.at[0, c, y], s_in.at[2 + t], r_in.at[2 + y], base + 2 * t + c)
    for g in range(2):
        push(kvh.at[4 + g], kvb.at[0, half, y % 2], s_in.at[6 + g], r_in.at[6 + y % 2], base + 2 * (2 * g + c) + half)
    place = 2 * (y % 2) + c
    for t in range(4):
        push(qh.at[t], qb.at[0, place], s_q.at[t], r_q.at[place], base + 2 * t + half)
        push(qh.at[4 + t // 2], qb.at[1, place], s_q.at[4 + t], r_q.at[4 + place], base + 2 * t + half)
        push(qh.at[6 + t // 2], qb.at[2, place], s_q.at[8 + t], r_q.at[8 + place], base + 2 * t + half)

    tails = []

    def ship(buf, ssem, rsem, target, cond=None):
        one = pltpu.make_async_remote_copy(
            src_ref=buf[0], dst_ref=buf[1], send_sem=ssem, recv_sem=rsem, device_id=(target, hd), device_id_type=MESH
        )
        if cond is None:
            one.start()
            tails.append((one, None))
        else:

            @pl.when(cond)
            def _():
                one.start()

            tails.append((one, cond))

    has_up = z < 7

    def hop_full(h):
        plane = (z + h) % 8
        mine = kvf.at[plane, c]
        if h == 0:
            for j in range(2):
                landed(kvf.at[plane, c, j], r_in.at[j])
        else:
            landed(mine, r_ff.at[h - 1])
        if h < 7:
            ship((mine, mine), s_ff.at[h], r_ff.at[h], down)
        if h == 0:
            ship((mine, mine), s_sf.at[h], r_sf.at[h], sib)
        else:
            ship((mine, mine), s_sf.at[h], r_sf.at[h], sib, plane < z)

    def hop_band(kv, n, first, s_f, r_f, s_s, r_s, d):
        mine = kv.at[d, c]
        if d == 0:
            for j in range(n):
                landed(kv.at[0, c, j], r_in.at[first + j])
            ship((mine, mine), s_s.at[0], r_s.at[0], sib)
            ship((mine, kv.at[1, c]), s_f.at[0], r_f.at[0], up, has_up)
        else:

            @pl.when(z >= d)
            def _():
                landed(mine, r_f.at[d - 1])

            ship((mine, mine), s_s.at[d], r_s.at[d], sib, z >= d)
            if d == 1:
                ship((mine, kv.at[2, c]), s_f.at[1], r_f.at[1], up, (z >= 1) & has_up)

    def band_a(d):
        hop_band(kva, 4, 2, s_fa, r_fa, s_sa, r_sa, d)

    def band_b(d):
        hop_band(kvb, 2, 6, s_fb, r_fb, s_sb, r_sb, d)

    hop_full(0)
    band_a(0)
    band_b(0)
    hop_full(1)
    hop_full(2)
    band_a(1)
    hop_full(3)
    band_b(1)
    hop_full(4)
    hop_full(5)
    band_a(2)
    hop_full(6)
    band_b(2)
    hop_full(7)

    for d in range(3):

        @pl.when(z >= d)
        def _():
            landed(kva.at[d, 1 - c], r_sa.at[d])
            landed(kvb.at[d, 1 - c], r_sb.at[d])

    for h in range(8):
        plane = (z + h) % 8

        @pl.when((plane < z) | (h == 0))
        def _():
            landed(kvf.at[plane, 1 - c], r_sf.at[h])

    for i in range(3):
        for j in range(4):
            landed(qb.at[i, j], r_q.at[4 * i + j])
    for one in sends:
        one.wait_send()
    for one, cond in tails:
        if cond is None:
            one.wait_send()
        else:

            @pl.when(cond)
            def _():
                one.wait_send()


def c_of(y):
    return y // 2


def exchange(qh, kvh):
    dma = pltpu.SemaphoreType.DMA
    counts = (8, 8, 12, 12, 2, 2, 2, 2, 7, 7, 3, 3, 3, 3, 8, 8)
    return pl.pallas_call(
        exchange_body,
        out_shape=(
            jax.ShapeDtypeStruct((3, 4, ROWS, HD), BF),
            jax.ShapeDtypeStruct((3, 2, 4, 2, ROWS, HD), BF),
            jax.ShapeDtypeStruct((3, 2, 2, 2, ROWS, HD), BF),
            jax.ShapeDtypeStruct((8, 2, 2, 2, ROWS, HD), BF),
        ),
        in_specs=[ANY, ANY],
        out_specs=(ANY, ANY, ANY, ANY),
        scratch_shapes=[dma((n,)) for n in counts],
        compiler_params=pltpu.CompilerParams(collective_id=0, has_side_effects=True),
        name="exchange",
    )(qh, kvh)


UNIT = 512


def attend_body(ids, spans, q, kva, kvb, kvf, o, lse, m_sc, l_sc, acc_sc):
    s, z, y, c, hd = position()
    pair, par = y // 2, y % 2
    here = 2 * z + c
    far = jnp.int32(1 << 20)

    def absorb(q_tile, k, v, q_first, k_first, reach):
        def scores():
            return SCALE2 * lax.dot_general(q_tile, k, (((1,), (1,)), ((), ())), preferred_element_type=F32)

        def update(sc):
            m_old = m_sc[...]
            m_new = jnp.maximum(m_old, jnp.max(sc, axis=1, keepdims=True))
            alpha = jnp.exp2(m_old - m_new)
            p = jnp.exp2(sc - jnp.tile(m_new, (1, UNIT // HD)))
            l_sc[...] = alpha * l_sc[...] + jnp.sum(p, axis=1, keepdims=True)
            acc_sc[...] = alpha * acc_sc[...] + jnp.dot(p.astype(BF), v, preferred_element_type=F32)
            m_sc[...] = m_new

        whole = (q_first >= k_first + 3 * ROWS - 1) & (q_first + ROWS - 1 - k_first < reach)

        @pl.when(whole)
        def _():
            update(scores())

        @pl.when(jnp.logical_not(whole))
        def _():
            row = lax.broadcasted_iota(jnp.int32, (ROWS, UNIT), 0)
            col = lax.broadcasted_iota(jnp.int32, (ROWS, UNIT), 1)
            gap = (q_first - k_first) + row - col - jnp.where(col >= ROWS, ROWS, 0)
            update(jnp.where((gap >= 0) & (gap < reach), scores(), FILL))

    def reset():
        m_sc[...] = jnp.full_like(m_sc, FLOOR)
        l_sc[...] = jnp.zeros_like(l_sc)
        acc_sc[...] = jnp.zeros_like(acc_sc)

    def store(t, which):
        l = l_sc[...]
        o[t, which] = (acc_sc[...] / jnp.where(l > 0.0, l, 1.0)).astype(BF)
        if which:
            total = jnp.where(l > 0.0, m_sc[...] + jnp.log2(jnp.where(l > 0.0, l, 1.0)), FILL)
            lse[t, which - 1] = total.T[:8]

    f0, f1 = ids[0], ids[1]
    reach_a = spans[pick(y, f0, f1)]
    reach_b = spans[pick(4 + pair, f0, f1)]

    def tile(t, _):
        q_first = (here * 4 + t) * ROWS

        def first_half(reach):
            return jnp.maximum(q_first - reach + 1, 0) // (4 * ROWS)

        reset()

        @pl.loop(2 * first_half(reach_a), 2 * here + 2)
        def _(n):
            hb, parity = n // 2, n % 2
            d, u = z - hb // 2, hb % 2
            absorb(
                q[0, t],
                kva[d, parity, pl.ds(2 * u, 2), 0].reshape(UNIT, HD),
                kva[d, parity, pl.ds(2 * u, 2), 1].reshape(UNIT, HD),
                q_first,
                hb * 4 * ROWS + parity * ROWS,
                reach_a,
            )

        store(t, 0)
        reset()

        @pl.loop(first_half(reach_b), here + 1)
        def _(hb):
            d, u = z - hb // 2, hb % 2
            absorb(
                q[1, t],
                kvb[d, u, :, 0].reshape(UNIT, HD),
                kvb[d, u, :, 1].reshape(UNIT, HD),
                q_first,
                hb * 4 * ROWS + par * ROWS,
                reach_b,
            )

        store(t, 1)
        reset()

        @pl.loop(0, here + 1)
        def _(hb):
            absorb(
                q[2, t],
                kvf[hb // 2, hb % 2, :, 0].reshape(UNIT, HD),
                kvf[hb // 2, hb % 2, :, 1].reshape(UNIT, HD),
                q_first,
                hb * 4 * ROWS + par * ROWS,
                far,
            )

        store(t, 2)
        return 0

    lax.fori_loop(0, 4, tile, 0)


def attend(local_ids, spans, qb, kva, kvb, kvf):
    return pl.pallas_call(
        attend_body,
        out_shape=(
            jax.ShapeDtypeStruct((4, 3, ROWS, HD), BF),
            jax.ShapeDtypeStruct((4, 2, 8, ROWS), F32),
        ),
        grid_spec=pltpu.PrefetchScalarGridSpec(
            num_scalar_prefetch=2,
            grid=(),
            in_specs=[VM] * 4,
            out_specs=[VM] * 2,
            scratch_shapes=[pltpu.VMEM((ROWS, HD), F32)] * 3,
        ),
        compiler_params=pltpu.CompilerParams(vmem_limit_bytes=40 << 20),
        name="attend",
    )(local_ids, spans, qb, kva, kvb, kvf)


def mix_body(ids, o, lse, w, out, wv, r, rl, merged, att, part, got, tmp, w_sem, s_o, r_o, s_l, r_l, s_x, r_x):
    s, z, y, c, hd = position()
    base = z * 8
    right, left = (hd + 1) % 4, (hd + 3) % 4
    pltpu.make_async_copy(w, wv, w_sem).start()
    greet(plane_peers(s, hd) + [(s, right), (s, left)])
    sends = []
    for t in range(4):
        home = base + 2 * (2 * c + t // 2) + t % 2
        for src, dst, ssem, rsem in ((o, r, s_o, r_o), (lse, rl, s_l, r_l)):
            one = Push(src.at[t], dst.at[y], ssem.at[t], rsem.at[y], home, s, hd)
            one.start()
            sends.append(one)
    for i in range(4):
        landed(r.at[i], r_o.at[i])
        landed(rl.at[i], r_l.at[i])
    for i in range(4):
        merged[i] = r[i, 0]
    for which in range(2):
        for pair in range(2):
            one, two = 2 * pair, 2 * pair + 1

            def column(i):
                return jnp.tile(rl[i, which], (16, 1)).T

            a, b = column(one), column(two)
            top = jnp.maximum(a, b)
            wa, wb = jnp.exp2(a - top), jnp.exp2(b - top)
            value = wa * r[one, which + 1].astype(F32) + wb * r[two, which + 1].astype(F32)
            merged[4 + 2 * which + pair] = (value / (wa + wb)).astype(BF)
    f0, f1 = ids[0], ids[1]
    for h in range(8):
        band = h - jnp.where(h > f0, 1, 0) - jnp.where(h > f1, 1, 0)
        slot = jnp.where(f0 == h, 6, jnp.where(f1 == h, 7, jnp.clip(band, 0, 5)))
        att[:, h * HD : (h + 1) * HD] = merged[slot]
    for one in sends:
        one.wait_send()
    landed(wv, w_sem)

    def project(dest):
        for half in range(2):
            for sub in range(2):
                columns = pl.ds(pl.multiple_of(dest * 1024 + half * 512 + sub * 256, 256), 256)
                piece = jnp.dot(att[...], wv[:, columns], preferred_element_type=F32)
                part[dest, half, :, sub * 256 : (sub + 1) * 256] = piece.astype(BF)

    def ship(src, slot, target):
        one = pltpu.make_async_remote_copy(
            src_ref=src,
            dst_ref=got.at[slot],
            send_sem=s_x.at[slot],
            recv_sem=r_x.at[slot],
            device_id=(s, target),
            device_id_type=MESH,
        )
        one.start()
        return one

    across = (hd + 2) % 4
    project(across)
    moved = [ship(part.at[across, 0], 0, right), ship(part.at[across, 1], 1, left)]
    project(right)
    moved.append(ship(part.at[right, 1], 2, right))
    project(left)
    moved.append(ship(part.at[left, 0], 3, left))
    landed(got.at[0], r_x.at[0])
    tmp[0] = (got[0].astype(F32) + part[right, 0].astype(F32)).astype(BF)
    moved.append(ship(tmp.at[0], 4, right))
    landed(got.at[1], r_x.at[1])
    tmp[1] = (got[1].astype(F32) + part[left, 1].astype(F32)).astype(BF)
    moved.append(ship(tmp.at[1], 5, left))
    project(hd)
    landed(got.at[2], r_x.at[2])
    landed(got.at[3], r_x.at[3])
    landed(got.at[4], r_x.at[4])
    out[:, :512] = (part[hd, 0].astype(F32) + got[4].astype(F32) + got[3].astype(F32)).astype(BF)
    landed(got.at[5], r_x.at[5])
    out[:, 512:] = (part[hd, 1].astype(F32) + got[5].astype(F32) + got[2].astype(F32)).astype(BF)
    for one in moved:
        one.wait_send()


def mix(local_ids, o, lse, w):
    dma = pltpu.SemaphoreType.DMA
    return pl.pallas_call(
        mix_body,
        out_shape=jax.ShapeDtypeStruct((ROWS, 1024), BF),
        in_specs=[pl.BlockSpec(memory_space=pltpu.SMEM), ANY, ANY, ANY],
        out_specs=VM,
        scratch_shapes=[
            pltpu.VMEM((1024, 4096), BF),
            pltpu.VMEM((4, 3, ROWS, HD), BF),
            pltpu.VMEM((4, 2, 8, ROWS), F32),
            pltpu.VMEM((8, ROWS, HD), BF),
            pltpu.VMEM((ROWS, 1024), BF),
            pltpu.VMEM((4, 2, ROWS, 512), BF),
            pltpu.VMEM((6, ROWS, 512), BF),
            pltpu.VMEM((2, ROWS, 512), BF),
            dma(()),
            dma((4,)),
            dma((4,)),
            dma((4,)),
            dma((4,)),
            dma((6,)),
            dma((6,)),
        ],
        compiler_params=pltpu.CompilerParams(collective_id=1, has_side_effects=True, vmem_limit_bytes=40 << 20),
        name="mix",
    )(local_ids, o, lse, w)


def on_device(queries, keys_in, values_in, out_weight, spans, full_ids):
    local_ids = full_ids - lax.axis_index("head") * 8
    qh, kvh = arrange(local_ids, queries, keys_in, values_in)
    qb, kva, kvb, kvf = exchange(qh, kvh)
    o, lse = attend(local_ids, spans, qb, kva, kvb, kvf)
    return mix(local_ids, o, lse, out_weight)


def solution(mesh):
    placed = (P("seq", "head"), P("seq", "head"), P("seq", "head"), P("head", None), P("head"), P("head"))
    return jax.shard_map(on_device, mesh=mesh, in_specs=placed, out_specs=P("seq", "head"), check_vma=False)
```

time: 739 us -> 183 us (0.25)
  the two profiles are of different devices: /device:TPU:25 before, /device:TPU:225 now
where the time goes in v1:
time: 183 us; the launch traced here: 182 us
  Pallas kernels  172 us (94%)
  local copies, waits for them, and re-layouts  8.74 us (5%)
    pallas_call x1, Pallas kernels, exchange(): pl.pallas_call(exchange_body, out_shape=(jax.ShapeDtypeStruct((3, 4, ROWS...  69.6 us
    pallas_call x1, Pallas kernels, attend(): pl.pallas_call(attend_body, out_shape=(jax.ShapeDtypeStruct((4, 3, ROWS,...  64.2 us
    pallas_call x1, Pallas kernels, mix(): pl.pallas_call(mix_body, out_shape=jax.ShapeDtypeStruct((ROWS, 1024), BF)...  32.2 us
    unnamed x15, local copies, waits for them, and re-layouts  8.74 us
    pallas_call x1, Pallas kernels, arrange(): pl.pallas_call(arrange_body, out_shape=(jax.ShapeDtypeStruct((8, ROWS, HD...  6.02 us

profile of v1, /device:TPU:225, one launch (start us, length us, event | category | flops | bytes accessed | tf_op | source)
XLA Modules:
  0.0 182.0 jit_solution(4489197867963151356)
XLA Ops:
  0.0 1.2 broadcast_subtract_fusion.ids
  1.2 6.0 %arrange.1 = (bf16[8,256,128]{2,1,0:T(8,128)(2,1)}, bf16[8,2,256,128]{3,2,1,0:T(8,128)(2,1)}) custom-call(s32[2]{0:T(128)} %broadcast_subtract_fusion.ids, bf16[256,1024]{1,0:T(8,128)(2,1)} %q.1, bf16[256,1024]{1,0:T(8,128)(2,1)} %k.1, bf16[256,1024]{1,0:T(8,128)(2,1)} %v.1), custom_call_target="tpu_custom_call" | custom-call | tf_op jit(solution)/shard_map/arrange/pallas_call | solution.py:50
  7.3 69.6 %exchange.1 = (bf16[3,4,256,128]{3,2,1,0:T(8,128)(2,1)}, bf16[3,2,4,2,256,128]{5,4,3,2,1,0:T(8,128)(2,1)}, bf16[3,2,2,2,256,128]{5,4,3,2,1,0:T(8,128)(2,1)}, bf16[8,2,2,2,256,128]{5,4,3,2,1,0:T(8,128)(2,1)}) custom-call(bf16[8,256,128]{2,1,0:T(8,128)(2,1)} %get-tuple-element.13.qh, bf16[8,2,256,128]{3,2,1,0:T(8,128)(2,1)} %get-tuple-element.14.kvh), custom_call_target="tpu_custom_call" | custom-call | tf_op jit(solution)/shard_map/exchange/pallas_call | solution.py:245
  76.9 0.0 copy-start.1
  76.9 2.2 %copy-done.1 = bf16[8,2,2,2,256,128]{5,4,3,2,1,0:T(8,128)(2,1)S(1)} copy-done((bf16[8,2,2,2,256,128]{5,4,3,2,1,0:T(8,128)(2,1)S(1)}, bf16[8,2,2,2,256,128]{5,4,3,2,1,0:T(8,128)(2,1)}, u32[]{:S(2)}) %copy-start.1) | copy-done | bytes 4194328
  79.1 0.0 copy-start.2
  79.1 1.9 %copy-done.2 = bf16[3,2,4,2,256,128]{5,4,3,2,1,0:T(8,128)(2,1)S(1)} copy-done((bf16[3,2,4,2,256,128]{5,4,3,2,1,0:T(8,128)(2,1)S(1)}, bf16[3,2,4,2,256,128]{5,4,3,2,1,0:T(8,128)(2,1)}, u32[]{:S(2)}) %copy-start.2) | copy-done | bytes 3145752
  81.0 0.0 copy-start.3
  81.0 1.4 copy-done.3
  82.4 0.0 copy-start.4
  82.4 1.1 copy-done.4
  83.5 0.0 copy-start.5
  83.5 0.7 copy-done.5
  84.2 0.0 copy-start.6
  84.2 0.7 copy-done.6
  84.9 0.0 copy-start
  84.9 64.2 %attend.1 = (bf16[4,3,256,128]{3,2,1,0:T(8,128)(2,1)S(1)}, f32[4,2,8,256]{3,2,1,0:T(8,128)S(1)}) custom-call(s32[2]{0:T(128)S(1)} %copy-done.5, s32[8]{0:T(128)S(1)} %copy-done.6, bf16[3,4,256,128]{3,2,1,0:T(8,128)(2,1)S(1)} %copy-done.4, bf16[3,2,4,2,256,128]{5,4,3,2,1,0:T(8,128)(2,1)S(1)} %copy-done.2, bf16[3,2,2,2,256,128]{5,4,3,2,1,0:T(8,128)(2,1)S(1)} %copy-done.3, ...), custom_call_target="tpu_custom_call" | custom-call | tf_op jit(solution)/shard_map/attend/pallas_call | solution.py:369
  149.0 0.0 copy-done
  149.0 32.2 %mix.1 = bf16[256,1024]{1,0:T(8,128)(2,1)S(1)} custom-call(s32[2]{0:T(128)S(1)} %copy-done.5, bf16[4,3,256,128]{3,2,1,0:T(8,128)(2,1)S(1)} %get-tuple-element.19.o, f32[4,2,8,256]{3,2,1,0:T(8,128)S(1)} %get-tuple-element.20.lse, bf16[1024,4096]{1,0:T(8,128)(2,1)S(1)} %copy-done), custom_call_target="tpu_custom_call" | custom-call | tf_op jit(solution)/shard_map/mix/pallas_call | solution.py:471
  181.3 0.8 copy.8
Async XLA Ops:
  76.9 2.2 %copy-start.1 = (bf16[8,2,2,2,256,128]{5,4,3,2,1,0:T(8,128)(2,1)S(1)}, bf16[8,2,2,2,256,128]{5,4,3,2,1,0:T(8,128)(2,1)}, u32[]{:S(2)}) copy-start(bf16[8,2,2,2,256,128]{5,4,3,2,1,0:T(8,128)(2,1)} %get-tuple-element.18.kvf) | copy-start | bytes 12582916
  79.1 1.9 %copy-start.2 = (bf16[3,2,4,2,256,128]{5,4,3,2,1,0:T(8,128)(2,1)S(1)}, bf16[3,2,4,2,256,128]{5,4,3,2,1,0:T(8,128)(2,1)}, u32[]{:S(2)}) copy-start(bf16[3,2,4,2,256,128]{5,4,3,2,1,0:T(8,128)(2,1)} %get-tuple-element.16.kva) | copy-start | bytes 9437188
  81.0 1.4 copy-start.3
  82.4 1.1 copy-start.4
  83.5 0.7 copy-start.5
  84.2 0.7 copy-start.6
  84.9 64.2 %copy-start = (bf16[1024,4096]{1,0:T(8,128)(2,1)S(1)}, bf16[1024,4096]{1,0:T(8,128)(2,1)}, u32[]{:S(2)}) copy-start(bf16[1024,4096]{1,0:T(8,128)(2,1)} %w.1) | copy-start | bytes 25165828

commit v2 on v1

v2 whole, which is shorter than its diff:
```python
import functools
import math

import jax
import jax.numpy as jnp
from jax import lax
from jax.experimental import pallas as pl
from jax.experimental.pallas import tpu as pltpu
from jax.sharding import PartitionSpec as P

HD = 128
ROWS = 256
SCALE2 = HD ** (-0.5) * math.log2(math.e)
FILL = -1e30
FLOOR = -5e29
MESH = pl.DeviceIdType.MESH
ANY = pl.BlockSpec(memory_space=pl.ANY)
VM = pl.BlockSpec(memory_space=pltpu.VMEM)
BF = jnp.bfloat16
F32 = jnp.float32


def position():
    s = lax.axis_index("seq")
    return s, s // 8, (s // 2) % 4, s % 2, lax.axis_index("head")


def pick(slot, f0, f1):
    h = slot + (slot >= f0).astype(jnp.int32)
    h = h + (h >= f1).astype(jnp.int32)
    return jnp.where(slot == 6, f0, jnp.where(slot == 7, f1, h))


def arrange_body(ids, q, k, v, qh, kvh):
    base = lax.axis_index("head") * 8
    f0, f1 = ids[0] - base, ids[1] - base
    for i in range(8):
        h = jnp.clip(pick(jnp.int32(i), f0, f1), 0, 7)
        columns = pl.ds(pl.multiple_of(h * HD, HD), HD)
        qh[i] = q[:, columns]
        kvh[i, 0] = k[:, columns]
        kvh[i, 1] = v[:, columns]


def arrange(full_ids, q, k, v):
    return pl.pallas_call(
        arrange_body,
        out_shape=(
            jax.ShapeDtypeStruct((8, ROWS, HD), BF),
            jax.ShapeDtypeStruct((8, 2, ROWS, HD), BF),
        ),
        in_specs=[pl.BlockSpec(memory_space=pltpu.SMEM), VM, VM, VM],
        out_specs=[VM, VM],
        name="arrange",
    )(full_ids, q, k, v)


def greet(targets):
    barrier = pltpu.get_barrier_semaphore()
    for target in targets:
        pl.semaphore_signal(barrier, inc=1, device_id=target, device_id_type=MESH)
    pl.semaphore_wait(barrier, len(targets))


def plane_peers(s, hd):
    base = (s // 8) * 8
    return [(base + (s + r) % 8, hd) for r in range(1, 8)]


class Push:
    def __init__(self, src, dst, ssem, rsem, target, me, hd):
        self.remote = pltpu.make_async_remote_copy(
            src_ref=src, dst_ref=dst, send_sem=ssem, recv_sem=rsem, device_id=(target, hd), device_id_type=MESH
        )
        self.local = pltpu.make_async_copy(src, dst, rsem)
        self.away = target != me

    def start(self):
        @pl.when(self.away)
        def _():
            self.remote.start()

        @pl.when(jnp.logical_not(self.away))
        def _():
            self.local.start()

    def wait_send(self):
        @pl.when(self.away)
        def _():
            self.remote.wait_send()


def landed(ref, sem):
    pltpu.make_async_copy(ref, ref, sem).wait()


TASKS = (
    (0, 0, 0),
    (0, 0, 1),
    (2, 0, 0),
    (1, 0, 0),
    (2, 1, 0),
    (0, 1, 0),
    (2, 2, 0),
    (0, 1, 1),
    (2, 3, 0),
    (1, 1, 0),
    (2, 4, 0),
    (0, 2, 0),
    (2, 5, 0),
    (0, 2, 1),
    (2, 6, 0),
    (1, 2, 0),
    (2, 7, 0),
)
MOVES = {
    1: (("f", 1),),
    2: (("b", 0), ("f", 2)),
    4: (("a", 1), ("f", 3)),
    6: (("f", 4),),
    8: (("b", 1), ("f", 5)),
    10: (("f", 6), ("a", 2)),
    12: (("f", 7),),
    13: (("b", 2),),
}


def table(n, values):
    out = jnp.int32(values[0])
    for i, value in enumerate(values[1:], 1):
        out = jnp.where(n == i, value, out)
    return out


def whole_body(
    ids, spans, qh, kvh, w, out,
    wv, kv, qb, o, lse, r, rl, merged, att, part, got, tmp, m_sc, l_sc, acc_sc, rel,
    w_sem, s_in, r_in, s_q, r_q, s_fa, r_fa, s_fb, r_fb, s_ff, r_ff, s_sa, r_sa, s_sb, r_sb, s_sf, r_sf,
    s_o, r_o, s_l, r_l, s_x, r_x,
):
    s, z, y, c, hd = position()
    pair, par = y // 2, y % 2
    base = z * 8
    up, down = (s + 8) % 64, (s + 56) % 64
    sib = base + 2 * y + (1 - c)
    right, left = (hd + 1) % 4, (hd + 3) % 4
    half = y // 2
    pltpu.make_async_copy(w, wv, w_sem).start()
    greet(plane_peers(s, hd) + [(up, hd), (down, hd), (s, right), (s, left)])

    sends = []

    def push(src, dst, ssem, rsem, target):
        one = Push(src, dst, ssem, rsem, target, s, hd)
        one.start()
        sends.append(one)

    def push_q(i, slot):
        for t in range(4):
            push(qh.at[slot(t)], qb.at[i, place], s_q.at[4 * i + t], r_q.at[4 * i + place], base + 2 * t + half)

    place = 2 * (y % 2) + c
    for g in range(2):
        push(kvh.at[6 + g], kv.at[9 + z, y], s_in.at[g], r_in.at[y % 2], base + 2 * (2 * g + c) + half)
    for t in range(4):
        push(kvh.at[t], kv.at[c, y], s_in.at[2 + t], r_in.at[2 + y], base + 2 * t + c)
    push_q(0, lambda t: t)
    push_q(2, lambda t: 6 + t // 2)
    for g in range(2):
        push(kvh.at[4 + g], kv.at[6, y], s_in.at[6 + g], r_in.at[6 + y % 2], base + 2 * (2 * g + c) + half)
    push_q(1, lambda t: 4 + t // 2)

    row = lax.broadcasted_iota(jnp.int32, (ROWS, 4 * ROWS), 0)
    col = lax.broadcasted_iota(jnp.int32, (ROWS, 4 * ROWS), 1)
    rel[...] = row - col - (col // ROWS) * ROWS
    m_sc[...] = jnp.full_like(m_sc, FLOOR)
    l_sc[...] = jnp.zeros_like(l_sc)
    acc_sc[...] = jnp.zeros_like(acc_sc)

    def hop(src, dst, ssem, rsem, target):
        return pltpu.make_async_remote_copy(
            src_ref=src, dst_ref=dst, send_sem=ssem, recv_sem=rsem, device_id=(target, hd), device_id_type=MESH
        )

    def when(cond, action):
        pl.when(cond)(action)

    mine2 = pl.ds(2 * c, 2)
    other2 = pl.ds(2 * (1 - c), 2)

    def full_down(h):
        ref = kv.at[9 + (z + h) % 8, mine2]
        return hop(ref, ref, s_ff.at[h], r_ff.at[h], down)

    def full_sib(h):
        ref = kv.at[9 + (z + h) % 8, mine2]
        return hop(ref, ref, s_sf.at[h], r_sf.at[h], sib)

    def needed(h):
        return z + h > 7 if h else z >= 0

    def move_full(h):
        if h == 0:
            for j in range(2):
                landed(kv.at[9 + z, 2 * c + j], r_in.at[j])
        else:
            landed(kv.at[9 + (z + h) % 8, mine2], r_ff.at[h - 1])
        if h < 7:
            full_down(h).start()
        when(needed(h), full_sib(h).start)

    def band_up(kind, d):
        if kind == "a":
            return hop(kv.at[2 * d + c], kv.at[2 * d + 2 + c], s_fa.at[d], r_fa.at[d], up)
        return hop(kv.at[6 + d, mine2], kv.at[7 + d, mine2], s_fb.at[d], r_fb.at[d], up)

    def band_sib(kind, d):
        if kind == "a":
            return hop(kv.at[2 * d + c], kv.at[2 * d + c], s_sa.at[d], r_sa.at[d], sib)
        return hop(kv.at[6 + d, mine2], kv.at[6 + d, mine2], s_sb.at[d], r_sb.at[d], sib)

    def move_band(kind, d):
        if d == 0 and kind == "a":
            for j in range(4):
                landed(kv.at[c, j], r_in.at[2 + j])
        elif d == 0:
            for j in range(2):
                landed(kv.at[6, 2 * c + j], r_in.at[6 + j])
        else:

            @pl.when(z >= d)
            def _():
                if kind == "a":
                    landed(kv.at[2 * d + c], r_fa.at[d - 1])
                else:
                    landed(kv.at[6 + d, mine2], r_fb.at[d - 1])

        if d < 2:
            when((z >= d) & (z < 7), band_up(kind, d).start)
        when(z >= d, band_sib(kind, d).start)

    move_full(0)
    move_band("a", 0)

    f0, f1 = ids[0] - hd * 8, ids[1] - hd * 8
    reach_a = spans[jnp.clip(pick(y, f0, f1), 0, 7)]
    reach_b = spans[jnp.clip(pick(4 + pair, f0, f1), 0, 7)]
    q_start = base * ROWS + c * 4 * ROWS

    def absorb(which, chunk, first, units, off, reach, masked):
        keys = units * ROWS
        k = kv[chunk, pl.ds(first, units), 0].reshape(keys, HD)
        v = kv[chunk, pl.ds(first, units), 1].reshape(keys, HD)

        def scores(t):
            sc = SCALE2 * lax.dot_general(
                qb[which, t], k, (((1,), (1,)), ((), ())), preferred_element_type=F32
            )
            if masked:
                at = rel[:, :keys]
                low = -(off + t * ROWS)
                sc = jnp.where((at >= low) & (at < low + reach), sc, FILL)
            return sc

        def soft(t, sc):
            m_old = m_sc[which, t]
            m_new = jnp.maximum(m_old, jnp.max(sc, axis=1, keepdims=True))
            alpha = jnp.exp2(m_old - m_new)
            p = jnp.exp2(sc - jnp.tile(m_new, (1, keys // HD)))
            m_sc[which, t] = m_new
            l_sc[which, t] = alpha * l_sc[which, t] + jnp.sum(p, axis=1, keepdims=True)
            return p.astype(BF), alpha

        def gather(t, p, alpha):
            acc_sc[which, t] = alpha * acc_sc[which, t] + jnp.dot(p, v, preferred_element_type=F32)

        current, pending = scores(0), None
        for t in range(4):
            following = scores(t + 1) if t < 3 else None
            weights = soft(t, current)
            if pending is not None:
                gather(*pending)
            pending = (t, *weights)
            current = following
        gather(*pending)

    def step(n, _):
        for at, moves in MOVES.items():

            @pl.when(n == at)
            def _(moves=moves):
                for kind, d in moves:
                    if kind == "f":
                        move_full(d)
                    else:
                        move_band(kind, d)

        for at, (which, d, other) in enumerate(TASKS):

            @pl.when(n == at)
            def _(which=which, d=d, other=other):
                if d == 0 and not other:
                    for j in range(4):
                        landed(qb.at[which, j], r_q.at[4 * which + j])
                if which == 0 and other:
                    when(z >= d, lambda: landed(kv.at[2 * d + 1 - c], r_sa.at[d]))
                if which == 1:
                    when(z >= d, lambda: landed(kv.at[6 + d, other2], r_sb.at[d]))
                if which == 2:
                    when(needed(d), lambda: landed(kv.at[9 + (z + d) % 8, other2], r_sf.at[d]))

        which = table(n, [t[0] for t in TASKS])
        d = table(n, [t[1] for t in TASKS])
        other = table(n, [t[2] for t in TASKS])
        side = jnp.where(other == 1, 1 - c, c)
        full = which == 2
        plane = jnp.where(full, (z + d) % 8, z - d)
        chunk = jnp.where(full, 9 + plane, jnp.where(which == 1, 6 + d, 2 * d + side))
        valid = jnp.where(full, (d == 0) | (plane < z), z >= d)
        parity = jnp.where(which == 0, side, par)
        off = q_start - plane * 8 * ROWS - parity * ROWS
        reach = jnp.where(full, 1 << 20, jnp.where(which == 1, reach_b, reach_a))
        lower = (d == 0) & (c == 0)
        upper = jnp.logical_not(full) & (d == 2) & (c == 1)
        plain = full & (d > 0)

        @pl.when(valid & plain)
        def _():
            absorb(which, chunk, 0, 4, off, reach, False)

        @pl.when(valid & jnp.logical_not(plain | lower | upper))
        def _():
            absorb(which, chunk, 0, 4, off, reach, True)

        @pl.when(valid & (lower | upper))
        def _():
            first = jnp.where(upper, 2, 0)
            absorb(which, chunk, first, 2, off - first * 2 * ROWS, reach, True)

        return 0

    lax.fori_loop(0, len(TASKS), step, 0)

    def send_back(t, _):
        for which in range(3):
            total = l_sc[which, t]
            safe = jnp.where(total > 0.0, total, 1.0)
            o[t, which] = (acc_sc[which, t] / safe).astype(BF)
            if which:
                level = jnp.where(total > 0.0, m_sc[which, t] + jnp.log2(safe), FILL)
                lse[t, which - 1] = level.T[:8]
        for back in backs(t):
            back.start()
        return 0

    def backs(t):
        home = base + 2 * (2 * c + t // 2) + t % 2
        return [
            Push(o.at[t], r.at[y], s_o.at[t], r_o.at[y], home, s, hd),
            Push(lse.at[t], rl.at[y], s_l.at[t], r_l.at[y], home, s, hd),
        ]

    lax.fori_loop(0, 4, send_back, 0)
    for i in range(4):
        landed(r.at[i], r_o.at[i])
        landed(rl.at[i], r_l.at[i])
    for i in range(4):
        merged[i] = r[i, 0]
    for which in range(2):
        for two in range(2):
            first, second = 2 * two, 2 * two + 1

            def column(i):
                return jnp.tile(rl[i, which], (16, 1)).T

            a, b = column(first), column(second)
            top = jnp.maximum(a, b)
            wa, wb = jnp.exp2(a - top), jnp.exp2(b - top)
            value = wa * r[first, which + 1].astype(F32) + wb * r[second, which + 1].astype(F32)
            merged[4 + 2 * which + two] = (value / (wa + wb)).astype(BF)
    for h in range(8):
        band = h - jnp.where(h > f0, 1, 0) - jnp.where(h > f1, 1, 0)
        slot = jnp.where(f0 == h, 6, jnp.where(f1 == h, 7, jnp.clip(band, 0, 5)))
        att[:, h * HD : (h + 1) * HD] = merged[slot]
    landed(wv, w_sem)

    def project(dest):
        for side in range(2):
            for sub in range(2):
                columns = pl.ds(pl.multiple_of(dest * 1024 + side * 512 + sub * 256, 256), 256)
                piece = jnp.dot(att[...], wv[:, columns], preferred_element_type=F32)
                part[dest, side, :, sub * 256 : (sub + 1) * 256] = piece.astype(BF)

    def ship(src, slot, target):
        one = pltpu.make_async_remote_copy(
            src_ref=src,
            dst_ref=got.at[slot],
            send_sem=s_x.at[slot],
            recv_sem=r_x.at[slot],
            device_id=(s, target),
            device_id_type=MESH,
        )
        one.start()
        return one

    across = (hd + 2) % 4
    project(across)
    moved = [ship(part.at[across, 0], 0, right), ship(part.at[across, 1], 1, left)]
    project(right)
    moved.append(ship(part.at[right, 1], 2, right))
    project(left)
    moved.append(ship(part.at[left, 0], 3, left))
    landed(got.at[0], r_x.at[0])
    tmp[0] = (got[0].astype(F32) + part[right, 0].astype(F32)).astype(BF)
    moved.append(ship(tmp.at[0], 4, right))
    landed(got.at[1], r_x.at[1])
    tmp[1] = (got[1].astype(F32) + part[left, 1].astype(F32)).astype(BF)
    moved.append(ship(tmp.at[1], 5, left))
    project(hd)
    for one in sends:
        one.wait_send()
    for h in range(7):
        full_down(h).wait_send()
    for h in range(8):
        when(needed(h), full_sib(h).wait_send)
    for kind in ("a", "b"):
        for d in range(3):
            if d < 2:
                when((z >= d) & (z < 7), band_up(kind, d).wait_send)
            when(z >= d, band_sib(kind, d).wait_send)
    for t in range(4):
        for back in backs(t):
            back.wait_send()
    landed(got.at[2], r_x.at[2])
    landed(got.at[3], r_x.at[3])
    landed(got.at[4], r_x.at[4])
    out[:, :512] = (part[hd, 0].astype(F32) + got[4].astype(F32) + got[3].astype(F32)).astype(BF)
    landed(got.at[5], r_x.at[5])
    out[:, 512:] = (part[hd, 1].astype(F32) + got[5].astype(F32) + got[2].astype(F32)).astype(BF)
    for one in moved:
        one.wait_send()


def whole(full_ids, spans, qh, kvh, w):
    dma = pltpu.SemaphoreType.DMA
    counts = (8, 8, 12, 12, 2, 2, 2, 2, 7, 7, 3, 3, 3, 3, 8, 8, 4, 4, 4, 4, 6, 6)
    smem = pl.BlockSpec(memory_space=pltpu.SMEM)
    return pl.pallas_call(
        whole_body,
        out_shape=jax.ShapeDtypeStruct((ROWS, 1024), BF),
        in_specs=[smem, smem, ANY, ANY, ANY],
        out_specs=VM,
        scratch_shapes=[
            pltpu.VMEM((1024, 4096), BF),
            pltpu.VMEM((17, 4, 2, ROWS, HD), BF),
            pltpu.VMEM((3, 4, ROWS, HD), BF),
            pltpu.VMEM((4, 3, ROWS, HD), BF),
            pltpu.VMEM((4, 2, 8, ROWS), F32),
            pltpu.VMEM((4, 3, ROWS, HD), BF),
            pltpu.VMEM((4, 2, 8, ROWS), F32),
            pltpu.VMEM((8, ROWS, HD), BF),
            pltpu.VMEM((ROWS, 1024), BF),
            pltpu.VMEM((4, 2, ROWS, 512), BF),
            pltpu.VMEM((6, ROWS, 512), BF),
            pltpu.VMEM((2, ROWS, 512), BF),
            pltpu.VMEM((3, 4, ROWS, HD), F32),
            pltpu.VMEM((3, 4, ROWS, HD), F32),
            pltpu.VMEM((3, 4, ROWS, HD), F32),
            pltpu.VMEM((ROWS, 4 * ROWS), jnp.int32),
            dma(()),
        ]
        + [dma((n,)) for n in counts],
        compiler_params=pltpu.CompilerParams(collective_id=0, has_side_effects=True, vmem_limit_bytes=56 << 20),
        name="whole",
    )(full_ids, spans, qh, kvh, w)


def on_device(queries, keys_in, values_in, out_weight, spans, full_ids):
    qh, kvh = arrange(full_ids, queries, keys_in, values_in)
    return whole(full_ids, spans, qh, kvh, out_weight)


def solution(mesh):
    placed = (P("seq", "head"), P("seq", "head"), P("seq", "head"), P("head", None), P("head"), P("head"))
    return jax.shard_map(on_device, mesh=mesh, in_specs=placed, out_specs=P("seq", "head"), check_vma=False)
```

time: 183 us -> 114 us (0.62)
  the two profiles are of different devices: /device:TPU:225 before, /device:TPU:97 now
where the time goes in v2:
time: 114 us
  Pallas kernels  112 us (98%)
  local copies, waits for them, and re-layouts  1.87 us (2%)
    pallas_call x1, Pallas kernels, whole(): pl.pallas_call(whole_body, out_shape=jax.ShapeDtypeStruct((ROWS, 1024), B...  109 us
    pallas_call x1, Pallas kernels, arrange(): pl.pallas_call(arrange_body, out_shape=(jax.ShapeDtypeStruct((8, ROWS, HD...  2.94 us

profile of v2, /device:TPU:97, one launch (start us, length us, event | category | flops | bytes accessed | tf_op | source)
XLA Modules:
  0.0 113.8 jit_solution(9515799870056059183)
XLA Ops:
  0.0 2.9 %arrange.1 = (bf16[8,256,128]{2,1,0:T(8,128)(2,1)}, bf16[8,2,256,128]{3,2,1,0:T(8,128)(2,1)}) custom-call(s32[2]{0:T(128)} %ids.3, bf16[256,1024]{1,0:T(8,128)(2,1)} %q.1, bf16[256,1024]{1,0:T(8,128)(2,1)} %k.1, bf16[256,1024]{1,0:T(8,128)(2,1)} %v.1), custom_call_target="tpu_custom_call" | custom-call | tf_op jit(solution)/shard_map/arrange/pallas_call | solution.py:46
  2.9 108.9 %whole.1 = bf16[256,1024]{1,0:T(8,128)(2,1)} custom-call(s32[2]{0:T(128)} %ids.3, s32[8]{0:T(128)} %spans.1, bf16[8,256,128]{2,1,0:T(8,128)(2,1)} %get-tuple-element.7.qh, bf16[8,2,256,128]{3,2,1,0:T(8,128)(2,1)} %get-tuple-element.8.kvh, bf16[1024,4096]{1,0:T(8,128)(2,1)} %w.1), custom_call_target="tpu_custom_call" | custom-call | tf_op jit(solution)/shard_map/whole/pallas_call | solution.py:448
  111.9 1.9 %copy.8 = bf16[256,1024]{1,0:T(8,128)(2,1)} copy(bf16[256,1024]{1,0:T(8,128)(2,1)} %whole.1) | data formatting | bytes 1048576

commit v3 on v2

--- a/solution.py
+++ b/solution.py
@@ -98,31 +98,22 @@
     (0, 0, 0),
     (0, 0, 1),
     (2, 0, 0),
+    (2, 1, 0),
     (1, 0, 0),
-    (2, 1, 0),
+    (2, 2, 0),
     (0, 1, 0),
-    (2, 2, 0),
+    (2, 3, 0),
     (0, 1, 1),
-    (2, 3, 0),
+    (2, 4, 0),
     (1, 1, 0),
-    (2, 4, 0),
+    (2, 5, 0),
     (0, 2, 0),
-    (2, 5, 0),
+    (2, 6, 0),
     (0, 2, 1),
-    (2, 6, 0),
     (1, 2, 0),
     (2, 7, 0),
 )
-MOVES = {
-    1: (("f", 1),),
-    2: (("b", 0), ("f", 2)),
-    4: (("a", 1), ("f", 3)),
-    6: (("f", 4),),
-    8: (("b", 1), ("f", 5)),
-    10: (("f", 6), ("a", 2)),
-    12: (("f", 7),),
-    13: (("b", 2),),
-}
+MOVES = {3: (("b", 0),), 4: (("a", 1),), 8: (("b", 1),), 11: (("a", 2),), 14: (("b", 2),)}
 
 
 def table(n, values):
@@ -160,22 +151,13 @@
             push(qh.at[slot(t)], qb.at[i, place], s_q.at[4 * i + t], r_q.at[4 * i + place], base + 2 * t + half)
 
     place = 2 * (y % 2) + c
-    for g in range(2):
-        push(kvh.at[6 + g], kv.at[9 + z, y], s_in.at[g], r_in.at[y % 2], base + 2 * (2 * g + c) + half)
-    for t in range(4):
-        push(kvh.at[t], kv.at[c, y], s_in.at[2 + t], r_in.at[2 + y], base + 2 * t + c)
-    push_q(0, lambda t: t)
-    push_q(2, lambda t: 6 + t // 2)
-    for g in range(2):
-        push(kvh.at[4 + g], kv.at[6, y], s_in.at[6 + g], r_in.at[6 + y % 2], base + 2 * (2 * g + c) + half)
-    push_q(1, lambda t: 4 + t // 2)
-
-    row = lax.broadcasted_iota(jnp.int32, (ROWS, 4 * ROWS), 0)
-    col = lax.broadcasted_iota(jnp.int32, (ROWS, 4 * ROWS), 1)
-    rel[...] = row - col - (col // ROWS) * ROWS
-    m_sc[...] = jnp.full_like(m_sc, FLOOR)
-    l_sc[...] = jnp.zeros_like(l_sc)
-    acc_sc[...] = jnp.zeros_like(acc_sc)
+    def prepare():
+        row = lax.broadcasted_iota(jnp.int32, (ROWS, 4 * ROWS), 0)
+        col = lax.broadcasted_iota(jnp.int32, (ROWS, 4 * ROWS), 1)
+        rel[...] = row - col - (col // ROWS) * ROWS
+        m_sc[...] = jnp.full_like(m_sc, FLOOR)
+        l_sc[...] = jnp.zeros_like(l_sc)
+        acc_sc[...] = jnp.zeros_like(acc_sc)
 
     def hop(src, dst, ssem, rsem, target):
         return pltpu.make_async_remote_copy(
@@ -188,9 +170,9 @@
     mine2 = pl.ds(2 * c, 2)
     other2 = pl.ds(2 * (1 - c), 2)
 
-    def full_down(h):
-        ref = kv.at[9 + (z + h) % 8, mine2]
-        return hop(ref, ref, s_ff.at[h], r_ff.at[h], down)
+    def full_down(h, j):
+        ref = kv.at[9 + (z + h) % 8, 2 * c + j]
+        return hop(ref, ref, s_ff.at[2 * h + j], r_ff.at[2 * h + j], down)
 
     def full_sib(h):
         ref = kv.at[9 + (z + h) % 8, mine2]
@@ -199,15 +181,13 @@
     def needed(h):
         return z + h > 7 if h else z >= 0
 
-    def move_full(h):
-        if h == 0:
-            for j in range(2):
-                landed(kv.at[9 + z, 2 * c + j], r_in.at[j])
-        else:
-            landed(kv.at[9 + (z + h) % 8, mine2], r_ff.at[h - 1])
+    def move_full(h, j):
+        ref = kv.at[9 + (z + h) % 8, 2 * c + j]
+        landed(ref, r_in.at[j] if h == 0 else r_ff.at[2 * h - 2 + j])
         if h < 7:
-            full_down(h).start()
-        when(needed(h), full_sib(h).start)
+            full_down(h, j).start()
+        if j == 1:
+            when(needed(h), full_sib(h).start)
 
     def band_up(kind, d):
         if kind == "a":
@@ -239,8 +219,22 @@
             when((z >= d) & (z < 7), band_up(kind, d).start)
         when(z >= d, band_sib(kind, d).start)
 
-    move_full(0)
+    for g in range(2):
+        push(kvh.at[6 + g], kv.at[9 + z, y], s_in.at[g], r_in.at[y % 2], base + 2 * (2 * g + c) + half)
+    prepare()
+    move_full(0, 0)
+    move_full(0, 1)
+    for t in range(4):
+        push(kvh.at[t], kv.at[c, y], s_in.at[2 + t], r_in.at[2 + y], base + 2 * t + c)
+    push_q(0, lambda t: t)
+    move_full(1, 0)
     move_band("a", 0)
+    push_q(2, lambda t: 6 + t // 2)
+    for g in range(2):
+        push(kvh.at[4 + g], kv.at[6, y], s_in.at[6 + g], r_in.at[6 + y % 2], base + 2 * (2 * g + c) + half)
+    move_full(1, 1)
+    move_full(2, 0)
+    push_q(1, lambda t: 4 + t // 2)
 
     f0, f1 = ids[0] - hd * 8, ids[1] - hd * 8
     reach_a = spans[jnp.clip(pick(y, f0, f1), 0, 7)]
@@ -285,15 +279,18 @@
         gather(*pending)
 
     def step(n, _):
+        for unit in range(5, 16):
+
+            @pl.when(n == unit - 4)
+            def _(unit=unit):
+                move_full(unit // 2, unit % 2)
+
         for at, moves in MOVES.items():
 
             @pl.when(n == at)
             def _(moves=moves):
                 for kind, d in moves:
-                    if kind == "f":
-                        move_full(d)
-                    else:
-                        move_band(kind, d)
+                    move_band(kind, d)
 
         for at, (which, d, other) in enumerate(TASKS):
 
@@ -420,7 +417,8 @@
     for one in sends:
         one.wait_send()
     for h in range(7):
-        full_down(h).wait_send()
+        for j in range(2):
+            full_down(h, j).wait_send()
     for h in range(8):
         when(needed(h), full_sib(h).wait_send)
     for kind in ("a", "b"):
@@ -443,7 +441,7 @@
 
 def whole(full_ids, spans, qh, kvh, w):
     dma = pltpu.SemaphoreType.DMA
-    counts = (8, 8, 12, 12, 2, 2, 2, 2, 7, 7, 3, 3, 3, 3, 8, 8, 4, 4, 4, 4, 6, 6)
+    counts = (8, 8, 12, 12, 2, 2, 2, 2, 14, 14, 3, 3, 3, 3, 8, 8, 4, 4, 4, 4, 6, 6)
     smem = pl.BlockSpec(memory_space=pltpu.SMEM)
     return pl.pallas_call(
         whole_body,

time: 114 us -> 107 us (0.939)
  Pallas kernels: 112 us -> 105 us
    pallas_call x1, Pallas kernels: 109 us -> 102 us  [whole(): pl.pallas_call(whole_body, out_shape=jax.ShapeDtypeStruct((ROWS, 1024), B...]
where the time goes in v3:
time: 107 us
  Pallas kernels  105 us (98%)
  local copies, waits for them, and re-layouts  1.87 us (2%)
    pallas_call x1, Pallas kernels, whole(): pl.pallas_call(whole_body, out_shape=jax.ShapeDtypeStruct((ROWS, 1024), B...  102 us
    pallas_call x1, Pallas kernels, arrange(): pl.pallas_call(arrange_body, out_shape=(jax.ShapeDtypeStruct((8, ROWS, HD...  2.94 us

profile of v3, /device:TPU:97, one launch (start us, length us, event | category | flops | bytes accessed | tf_op | source)
XLA Modules:
  0.0 106.8 jit_solution(17828938457644325087)
XLA Ops:
  0.0 2.9 %arrange.1 = (bf16[8,256,128]{2,1,0:T(8,128)(2,1)}, bf16[8,2,256,128]{3,2,1,0:T(8,128)(2,1)}) custom-call(s32[2]{0:T(128)} %ids.3, bf16[256,1024]{1,0:T(8,128)(2,1)} %q.1, bf16[256,1024]{1,0:T(8,128)(2,1)} %k.1, bf16[256,1024]{1,0:T(8,128)(2,1)} %v.1), custom_call_target="tpu_custom_call" | custom-call | tf_op jit(solution)/shard_map/arrange/pallas_call | solution.py:46
  2.9 102.0 %whole.1 = bf16[256,1024]{1,0:T(8,128)(2,1)} custom-call(s32[2]{0:T(128)} %ids.3, s32[8]{0:T(128)} %spans.1, bf16[8,256,128]{2,1,0:T(8,128)(2,1)} %get-tuple-element.7.qh, bf16[8,2,256,128]{3,2,1,0:T(8,128)(2,1)} %get-tuple-element.8.kvh, bf16[1024,4096]{1,0:T(8,128)(2,1)} %w.1), custom_call_target="tpu_custom_call" | custom-call | tf_op jit(solution)/shard_map/whole/pallas_call | solution.py:446
  104.9 1.9 %copy.8 = bf16[256,1024]{1,0:T(8,128)(2,1)} copy(bf16[256,1024]{1,0:T(8,128)(2,1)} %whole.1) | data formatting | bytes 1048576

commit v4 on v3

--- a/solution.py
+++ b/solution.py
@@ -29,30 +29,6 @@
     h = slot + (slot >= f0).astype(jnp.int32)
     h = h + (h >= f1).astype(jnp.int32)
     return jnp.where(slot == 6, f0, jnp.where(slot == 7, f1, h))
-
-
-def arrange_body(ids, q, k, v, qh, kvh):
-    base = lax.axis_index("head") * 8
-    f0, f1 = ids[0] - base, ids[1] - base
-    for i in range(8):
-        h = jnp.clip(pick(jnp.int32(i), f0, f1), 0, 7)
-        columns = pl.ds(pl.multiple_of(h * HD, HD), HD)
-        qh[i] = q[:, columns]
-        kvh[i, 0] = k[:, columns]
-        kvh[i, 1] = v[:, columns]
-
-
-def arrange(full_ids, q, k, v):
-    return pl.pallas_call(
-        arrange_body,
-        out_shape=(
-            jax.ShapeDtypeStruct((8, ROWS, HD), BF),
-            jax.ShapeDtypeStruct((8, 2, ROWS, HD), BF),
-        ),
-        in_specs=[pl.BlockSpec(memory_space=pltpu.SMEM), VM, VM, VM],
-        out_specs=[VM, VM],
-        name="arrange",
-    )(full_ids, q, k, v)
 
 
 def greet(targets):
@@ -108,12 +84,13 @@
     (1, 1, 0),
     (2, 5, 0),
     (0, 2, 0),
+    (0, 2, 1),
     (2, 6, 0),
-    (0, 2, 1),
     (1, 2, 0),
     (2, 7, 0),
 )
-MOVES = {3: (("b", 0),), 4: (("a", 1),), 8: (("b", 1),), 11: (("a", 2),), 14: (("b", 2),)}
+MOVES = {3: (("b", 0),), 4: (("a", 1),), 8: (("b", 1),), 12: (("a", 2),), 14: (("b", 2),)}
+DONE = {14: 0, 16: 1}
 
 
 def table(n, values):
@@ -124,8 +101,8 @@
 
 
 def whole_body(
-    ids, spans, qh, kvh, w, out,
-    wv, kv, qb, o, lse, r, rl, merged, att, part, got, tmp, m_sc, l_sc, acc_sc, rel,
+    ids, spans, queries, keys_in, values_in, w, out,
+    qh, kvh, wv, kv, qb, o, lse, r, rl, merged, att, part, got, tmp, m_sc, l_sc, acc_sc, rel,
     w_sem, s_in, r_in, s_q, r_q, s_fa, r_fa, s_fb, r_fb, s_ff, r_ff, s_sa, r_sa, s_sb, r_sb, s_sf, r_sf,
     s_o, r_o, s_l, r_l, s_x, r_x,
 ):
@@ -137,7 +114,28 @@
     right, left = (hd + 1) % 4, (hd + 3) % 4
     half = y // 2
     pltpu.make_async_copy(w, wv, w_sem).start()
-    greet(plane_peers(s, hd) + [(up, hd), (down, hd), (s, right), (s, left)])
+    f0, f1 = ids[0] - hd * 8, ids[1] - hd * 8
+
+    def column_of(ref, slot):
+        h = pick(jnp.int32(slot), f0, f1)
+        first, last = (slot, slot + 2) if slot < 6 else (slot - 6, slot)
+        out = ref[:, last * HD : (last + 1) * HD]
+        for i in range(first, last):
+            out = jnp.where(h == i, ref[:, i * HD : (i + 1) * HD], out)
+        return out
+
+    def arrange_kv(slots):
+        for i in slots:
+            kvh[i, 0] = column_of(keys_in, i)
+            kvh[i, 1] = column_of(values_in, i)
+
+    def arrange_q(slots):
+        for i in slots:
+            qh[i] = column_of(queries, i)
+
+    arrange_kv((6, 7))
+    opposite = [((7 - z) * 8 + i, hd) for i in range(8)]
+    greet(plane_peers(s, hd) + [(up, hd), (down, hd), (s, right), (s, left)] + opposite)
 
     sends = []
 
@@ -148,7 +146,8 @@
 
     def push_q(i, slot):
         for t in range(4):
-            push(qh.at[slot(t)], qb.at[i, place], s_q.at[4 * i + t], r_q.at[4 * i + place], base + 2 * t + half)
+            there = jnp.where(c == 1, 7 - z, z) * 8 if i == 2 else base
+            push(qh.at[slot(t)], qb.at[i, place], s_q.at[4 * i + t], r_q.at[4 * i + place], there + 2 * t + half)
 
     place = 2 * (y % 2) + c
     def prepare():
@@ -179,7 +178,7 @@
         return hop(ref, ref, s_sf.at[h], r_sf.at[h], sib)
 
     def needed(h):
-        return z + h > 7 if h else z >= 0
+        return (z + h) % 8 <= jnp.maximum(z, 7 - z)
 
     def move_full(h, j):
         ref = kv.at[9 + (z + h) % 8, 2 * c + j]
@@ -221,12 +220,16 @@
 
     for g in range(2):
         push(kvh.at[6 + g], kv.at[9 + z, y], s_in.at[g], r_in.at[y % 2], base + 2 * (2 * g + c) + half)
-    prepare()
+    arrange_kv(range(4))
+    arrange_q(range(4))
     move_full(0, 0)
     move_full(0, 1)
     for t in range(4):
         push(kvh.at[t], kv.at[c, y], s_in.at[2 + t], r_in.at[2 + y], base + 2 * t + c)
     push_q(0, lambda t: t)
+    arrange_kv((4, 5))
+    arrange_q(range(4, 8))
+    prepare()
     move_full(1, 0)
     move_band("a", 0)
     push_q(2, lambda t: 6 + t // 2)
@@ -236,12 +239,11 @@
     move_full(2, 0)
     push_q(1, lambda t: 4 + t // 2)
 
-    f0, f1 = ids[0] - hd * 8, ids[1] - hd * 8
     reach_a = spans[jnp.clip(pick(y, f0, f1), 0, 7)]
     reach_b = spans[jnp.clip(pick(4 + pair, f0, f1), 0, 7)]
     q_start = base * ROWS + c * 4 * ROWS
 
-    def absorb(which, chunk, first, units, off, reach, masked):
+    def absorb(which, chunk, first, units, tiles, off, skew, reach, masked):
         keys = units * ROWS
         k = kv[chunk, pl.ds(first, units), 0].reshape(keys, HD)
         v = kv[chunk, pl.ds(first, units), 1].reshape(keys, HD)
@@ -252,7 +254,7 @@
             )
             if masked:
                 at = rel[:, :keys]
-                low = -(off + t * ROWS)
+                low = -(off + t * ROWS + (t % 2) * skew)
                 sc = jnp.where((at >= low) & (at < low + reach), sc, FILL)
             return sc
 
@@ -268,9 +270,9 @@
         def gather(t, p, alpha):
             acc_sc[which, t] = alpha * acc_sc[which, t] + jnp.dot(p, v, preferred_element_type=F32)
 
-        current, pending = scores(0), None
-        for t in range(4):
-            following = scores(t + 1) if t < 3 else None
+        current, pending = scores(tiles[0]), None
+        for i, t in enumerate(tiles):
+            following = scores(tiles[i + 1]) if i + 1 < len(tiles) else None
             weights = soft(t, current)
             if pending is not None:
                 gather(*pending)
@@ -291,6 +293,12 @@
             def _(moves=moves):
                 for kind, d in moves:
                     move_band(kind, d)
+
+        for at, which in DONE.items():
+
+            @pl.when(n == at)
+            def _(which=which):
+                send_back(which)
 
         for at, (which, d, other) in enumerate(TASKS):
 
@@ -313,67 +321,86 @@
         full = which == 2
         plane = jnp.where(full, (z + d) % 8, z - d)
         chunk = jnp.where(full, 9 + plane, jnp.where(which == 1, 6 + d, 2 * d + side))
-        valid = jnp.where(full, (d == 0) | (plane < z), z >= d)
+        own, mirror = plane <= z, plane <= 7 - z
+        quad = jnp.where(full, own & mirror, z >= d)
+        pair_only = full & (own != mirror)
         parity = jnp.where(which == 0, side, par)
         off = q_start - plane * 8 * ROWS - parity * ROWS
         reach = jnp.where(full, 1 << 20, jnp.where(which == 1, reach_b, reach_a))
-        lower = (d == 0) & (c == 0)
+        skew = jnp.where(full, (7 - 2 * z) * 8 * ROWS, 0)
+        lower = jnp.logical_not(full) & (d == 0) & (c == 0)
         upper = jnp.logical_not(full) & (d == 2) & (c == 1)
-        plain = full & (d > 0)
-
-        @pl.when(valid & plain)
-        def _():
-            absorb(which, chunk, 0, 4, off, reach, False)
-
-        @pl.when(valid & jnp.logical_not(plain | lower | upper))
-        def _():
-            absorb(which, chunk, 0, 4, off, reach, True)
-
-        @pl.when(valid & (lower | upper))
+        plain = full & (plane != z) & (plane != 7 - z)
+        four = (0, 1, 2, 3)
+
+        @pl.when(quad & plain)
+        def _():
+            absorb(which, chunk, 0, 4, four, off, skew, reach, False)
+
+        @pl.when(quad & jnp.logical_not(plain | lower | upper))
+        def _():
+            absorb(which, chunk, 0, 4, four, off, skew, reach, True)
+
+        @pl.when(quad & (lower | upper))
         def _():
             first = jnp.where(upper, 2, 0)
-            absorb(which, chunk, first, 2, off - first * 2 * ROWS, reach, True)
+            absorb(which, chunk, first, 2, four, off - first * 2 * ROWS, skew, reach, True)
+
+        start = jnp.where(own, 0, 1)
+
+        @pl.when(pair_only & plain)
+        def _():
+            absorb(which, chunk, 0, 4, (start, start + 2), off, skew, reach, False)
+
+        @pl.when(pair_only & jnp.logical_not(plain))
+        def _():
+            absorb(which, chunk, 0, 4, (start, start + 2), off, skew, reach, True)
 
         return 0
 
-    lax.fori_loop(0, len(TASKS), step, 0)
-
-    def send_back(t, _):
-        for which in range(3):
+    def backs(which, t):
+        there = jnp.where(t % 2 == 1, 7 - z, z) * 8 if which == 2 else base
+        home = there + 2 * (2 * c + t // 2) + t % 2
+        i = 4 * which
+        out = [Push(o.at[which, t], r.at[which, y], s_o.at[i + t], r_o.at[i + y], home, s, hd)]
+        if which:
+            i -= 4
+            out.append(Push(lse.at[which - 1, t], rl.at[which - 1, y], s_l.at[i + t], r_l.at[i + y], home, s, hd))
+        return out
+
+    def send_back(which):
+        def one(t, _):
             total = l_sc[which, t]
             safe = jnp.where(total > 0.0, total, 1.0)
-            o[t, which] = (acc_sc[which, t] / safe).astype(BF)
+            o[which, t] = (acc_sc[which, t] / safe).astype(BF)
             if which:
                 level = jnp.where(total > 0.0, m_sc[which, t] + jnp.log2(safe), FILL)
-                lse[t, which - 1] = level.T[:8]
-        for back in backs(t):
-            back.start()
-        return 0
-
-    def backs(t):
-        home = base + 2 * (2 * c + t // 2) + t % 2
-        return [
-            Push(o.at[t], r.at[y], s_o.at[t], r_o.at[y], home, s, hd),
-            Push(lse.at[t], rl.at[y], s_l.at[t], r_l.at[y], home, s, hd),
-        ]
-
-    lax.fori_loop(0, 4, send_back, 0)
+                lse[which - 1, t] = level.T[:8]
+            for back in backs(which, t):
+                back.start()
+            return 0
+
+        lax.fori_loop(0, 4, one, 0)
+
+    lax.fori_loop(0, len(TASKS), step, 0)
+    send_back(2)
     for i in range(4):
-        landed(r.at[i], r_o.at[i])
-        landed(rl.at[i], r_l.at[i])
-    for i in range(4):
-        merged[i] = r[i, 0]
+        landed(r.at[0, i], r_o.at[i])
+        merged[i] = r[0, i]
     for which in range(2):
+        for i in range(4):
+            landed(r.at[which + 1, i], r_o.at[4 * which + 4 + i])
+            landed(rl.at[which, i], r_l.at[4 * which + i])
         for two in range(2):
             first, second = 2 * two, 2 * two + 1
 
             def column(i):
-                return jnp.tile(rl[i, which], (16, 1)).T
+                return jnp.tile(rl[which, i], (16, 1)).T
 
             a, b = column(first), column(second)
             top = jnp.maximum(a, b)
             wa, wb = jnp.exp2(a - top), jnp.exp2(b - top)
-            value = wa * r[first, which + 1].astype(F32) + wb * r[second, which + 1].astype(F32)
+            value = wa * r[which + 1, first].astype(F32) + wb * r[which + 1, second].astype(F32)
             merged[4 + 2 * which + two] = (value / (wa + wb)).astype(BF)
     for h in range(8):
         band = h - jnp.where(h > f0, 1, 0) - jnp.where(h > f1, 1, 0)
@@ -426,9 +453,10 @@
             if d < 2:
                 when((z >= d) & (z < 7), band_up(kind, d).wait_send)
             when(z >= d, band_sib(kind, d).wait_send)
-    for t in range(4):
-        for back in backs(t):
-            back.wait_send()
+    for which in range(3):
+        for t in range(4):
+            for back in backs(which, t):
+                back.wait_send()
     landed(got.at[2], r_x.at[2])
     landed(got.at[3], r_x.at[3])
     landed(got.at[4], r_x.at[4])
@@ -439,23 +467,25 @@
         one.wait_send()
 
 
-def whole(full_ids, spans, qh, kvh, w):
+def whole(full_ids, spans, queries, keys_in, values_in, w):
     dma = pltpu.SemaphoreType.DMA
-    counts = (8, 8, 12, 12, 2, 2, 2, 2, 14, 14, 3, 3, 3, 3, 8, 8, 4, 4, 4, 4, 6, 6)
+    counts = (8, 8, 12, 12, 2, 2, 2, 2, 14, 14, 3, 3, 3, 3, 8, 8, 12, 12, 8, 8, 6, 6)
     smem = pl.BlockSpec(memory_space=pltpu.SMEM)
     return pl.pallas_call(
         whole_body,
         out_shape=jax.ShapeDtypeStruct((ROWS, 1024), BF),
-        in_specs=[smem, smem, ANY, ANY, ANY],
+        in_specs=[smem, smem, VM, VM, VM, ANY],
         out_specs=VM,
         scratch_shapes=[
+            pltpu.VMEM((8, ROWS, HD), BF),
+            pltpu.VMEM((8, 2, ROWS, HD), BF),
             pltpu.VMEM((1024, 4096), BF),
             pltpu.VMEM((17, 4, 2, ROWS, HD), BF),
             pltpu.VMEM((3, 4, ROWS, HD), BF),
-            pltpu.VMEM((4, 3, ROWS, HD), BF),
-            pltpu.VMEM((4, 2, 8, ROWS), F32),
-            pltpu.VMEM((4, 3, ROWS, HD), BF),
-            pltpu.VMEM((4, 2, 8, ROWS), F32),
+            pltpu.VMEM((3, 4, ROWS, HD), BF),
+            pltpu.VMEM((2, 4, 8, ROWS), F32),
+            pltpu.VMEM((3, 4, ROWS, HD), BF),
+            pltpu.VMEM((2, 4, 8, ROWS), F32),
             pltpu.VMEM((8, ROWS, HD), BF),
             pltpu.VMEM((ROWS, 1024), BF),
             pltpu.VMEM((4, 2, ROWS, 512), BF),
@@ -470,12 +500,11 @@
         + [dma((n,)) for n in counts],
         compiler_params=pltpu.CompilerParams(collective_id=0, has_side_effects=True, vmem_limit_bytes=56 << 20),
         name="whole",
-    )(full_ids, spans, qh, kvh, w)
+    )(full_ids, spans, queries, keys_in, values_in, w)
 
 
 def on_device(queries, keys_in, values_in, out_weight, spans, full_ids):
-    qh, kvh = arrange(full_ids, queries, keys_in, values_in)
-    return whole(full_ids, spans, qh, kvh, out_weight)
+    return whole(full_ids, spans, queries, keys_in, values_in, out_weight)
 
 
 def solution(mesh):

time: 107 us -> 112 us (1.047); the launches traced: 107 us -> 110 us
  Pallas kernels: 105 us -> 108 us
    pallas_call x1, Pallas kernels: 102 us -> 108 us  [whole(): pl.pallas_call(whole_body, out_shape=jax.ShapeDtypeStruct((ROWS, 1024), B...]
    pallas_call x1 -> x0, Pallas kernels: 2.94 us -> none  [arrange(): pl.pallas_call(arrange_body, out_shape=(jax.ShapeDtypeStruct((8, ROWS, HD...]
where the time goes in v4:
time: 112 us; the launch traced here: 110 us
  Pallas kernels  108 us (96%)
  local copies, waits for them, and re-layouts  1.87 us (2%)
    pallas_call x1, Pallas kernels, whole(): pl.pallas_call(whole_body, out_shape=jax.ShapeDtypeStruct((ROWS, 1024), B...  108 us

profile of v4, /device:TPU:97, one launch (start us, length us, event | category | flops | bytes accessed | tf_op | source)
XLA Modules:
  0.0 110.2 jit_solution(7051232849413579576)
XLA Ops:
  0.0 108.4 %whole.1 = bf16[256,1024]{1,0:T(8,128)(2,1)} custom-call(s32[2]{0:T(128)} %ids.1, s32[8]{0:T(128)} %spans.1, bf16[256,1024]{1,0:T(8,128)(2,1)} %queries.1, bf16[256,1024]{1,0:T(8,128)(2,1)} %keys_in.1, bf16[256,1024]{1,0:T(8,128)(2,1)} %values_in.1, bf16[1024,4096]{1,0:T(8,128)(2,1)} %w.1), custom_call_target="tpu_custom_call" | custom-call | tf_op jit(solution)/shard_map/whole/pallas_call | solution.py:474
  108.4 1.9 %copy.8 = bf16[256,1024]{1,0:T(8,128)(2,1)} copy(bf16[256,1024]{1,0:T(8,128)(2,1)} %whole.1) | data formatting | bytes 1048576

commit v5 on v4

--- a/solution.py
+++ b/solution.py
@@ -74,23 +74,23 @@
     (0, 0, 0),
     (0, 0, 1),
     (2, 0, 0),
+    (2, 7, 0),
+    (1, 0, 0),
     (2, 1, 0),
-    (1, 0, 0),
+    (0, 1, 0),
     (2, 2, 0),
-    (0, 1, 0),
+    (0, 1, 1),
     (2, 3, 0),
-    (0, 1, 1),
+    (1, 1, 0),
     (2, 4, 0),
-    (1, 1, 0),
     (2, 5, 0),
     (0, 2, 0),
+    (2, 6, 0),
     (0, 2, 1),
-    (2, 6, 0),
     (1, 2, 0),
-    (2, 7, 0),
 )
-MOVES = {3: (("b", 0),), 4: (("a", 1),), 8: (("b", 1),), 12: (("a", 2),), 14: (("b", 2),)}
-DONE = {14: 0, 16: 1}
+MOVES = {2: (("f", 7),), 3: (("b", 0),), 4: (("a", 1),), 8: (("b", 1),), 12: (("a", 2),), 15: (("b", 2),)}
+DONE = {15: 2, 16: 0}
 
 
 def table(n, values):
@@ -103,7 +103,7 @@
 def whole_body(
     ids, spans, queries, keys_in, values_in, w, out,
     qh, kvh, wv, kv, qb, o, lse, r, rl, merged, att, part, got, tmp, m_sc, l_sc, acc_sc, rel,
-    w_sem, s_in, r_in, s_q, r_q, s_fa, r_fa, s_fb, r_fb, s_ff, r_ff, s_sa, r_sa, s_sb, r_sb, s_sf, r_sf,
+    w_sem, s_in, r_in, s_q, r_q, s_fa, r_fa, s_fb, r_fb, s_ff, r_ff, s_fu, r_fu, s_sa, r_sa, s_sb, r_sb, s_sf, r_sf,
     s_o, r_o, s_l, r_l, s_x, r_x,
 ):
     s, z, y, c, hd = position()
@@ -134,8 +134,7 @@
             qh[i] = column_of(queries, i)
 
     arrange_kv((6, 7))
-    opposite = [((7 - z) * 8 + i, hd) for i in range(8)]
-    greet(plane_peers(s, hd) + [(up, hd), (down, hd), (s, right), (s, left)] + opposite)
+    greet(plane_peers(s, hd) + [(up, hd), (down, hd), (s, right), (s, left)])
 
     sends = []
 
@@ -146,8 +145,7 @@
 
     def push_q(i, slot):
         for t in range(4):
-            there = jnp.where(c == 1, 7 - z, z) * 8 if i == 2 else base
-            push(qh.at[slot(t)], qb.at[i, place], s_q.at[4 * i + t], r_q.at[4 * i + place], there + 2 * t + half)
+            push(qh.at[slot(t)], qb.at[i, place], s_q.at[4 * i + t], r_q.at[4 * i + place], base + 2 * t + half)
 
     place = 2 * (y % 2) + c
     def prepare():
@@ -178,13 +176,19 @@
         return hop(ref, ref, s_sf.at[h], r_sf.at[h], sib)
 
     def needed(h):
-        return (z + h) % 8 <= jnp.maximum(z, 7 - z)
+        return (z + h) % 8 <= z
+
+    def full_up(j):
+        ref = kv.at[9 + z, 2 * c + j]
+        return hop(ref, ref, s_fu.at[j], r_fu.at[j], up)
 
     def move_full(h, j):
         ref = kv.at[9 + (z + h) % 8, 2 * c + j]
-        landed(ref, r_in.at[j] if h == 0 else r_ff.at[2 * h - 2 + j])
-        if h < 7:
+        landed(ref, r_in.at[j] if h == 0 else r_fu.at[j] if h == 7 else r_ff.at[2 * h - 2 + j])
+        if h < 6:
             full_down(h, j).start()
+        if h == 0:
+            full_up(j).start()
         if j == 1:
             when(needed(h), full_sib(h).start)
 
@@ -243,7 +247,7 @@
     reach_b = spans[jnp.clip(pick(4 + pair, f0, f1), 0, 7)]
     q_start = base * ROWS + c * 4 * ROWS
 
-    def absorb(which, chunk, first, units, tiles, off, skew, reach, masked):
+    def absorb(which, chunk, first, units, off, reach, masked):
         keys = units * ROWS
         k = kv[chunk, pl.ds(first, units), 0].reshape(keys, HD)
         v = kv[chunk, pl.ds(first, units), 1].reshape(keys, HD)
@@ -254,7 +258,7 @@
             )
             if masked:
                 at = rel[:, :keys]
-                low = -(off + t * ROWS + (t % 2) * skew)
+                low = -(off + t * ROWS)
                 sc = jnp.where((at >= low) & (at < low + reach), sc, FILL)
             return sc
 
@@ -270,9 +274,9 @@
         def gather(t, p, alpha):
             acc_sc[which, t] = alpha * acc_sc[which, t] + jnp.dot(p, v, preferred_element_type=F32)
 
-        current, pending = scores(tiles[0]), None
-        for i, t in enumerate(tiles):
-            following = scores(tiles[i + 1]) if i + 1 < len(tiles) else None
+        current, pending = scores(0), None
+        for t in range(4):
+            following = scores(t + 1) if t < 3 else None
             weights = soft(t, current)
             if pending is not None:
                 gather(*pending)
@@ -281,7 +285,7 @@
         gather(*pending)
 
     def step(n, _):
-        for unit in range(5, 16):
+        for unit in range(5, 14):
 
             @pl.when(n == unit - 4)
             def _(unit=unit):
@@ -292,7 +296,11 @@
             @pl.when(n == at)
             def _(moves=moves):
                 for kind, d in moves:
-                    move_band(kind, d)
+                    if kind == "f":
+                        move_full(d, 0)
+                        move_full(d, 1)
+                    else:
+                        move_band(kind, d)
 
         for at, which in DONE.items():
 
@@ -321,46 +329,31 @@
         full = which == 2
         plane = jnp.where(full, (z + d) % 8, z - d)
         chunk = jnp.where(full, 9 + plane, jnp.where(which == 1, 6 + d, 2 * d + side))
-        own, mirror = plane <= z, plane <= 7 - z
-        quad = jnp.where(full, own & mirror, z >= d)
-        pair_only = full & (own != mirror)
+        valid = jnp.where(full, plane <= z, z >= d)
         parity = jnp.where(which == 0, side, par)
         off = q_start - plane * 8 * ROWS - parity * ROWS
         reach = jnp.where(full, 1 << 20, jnp.where(which == 1, reach_b, reach_a))
-        skew = jnp.where(full, (7 - 2 * z) * 8 * ROWS, 0)
-        lower = jnp.logical_not(full) & (d == 0) & (c == 0)
+        lower = (d == 0) & (c == 0)
         upper = jnp.logical_not(full) & (d == 2) & (c == 1)
-        plain = full & (plane != z) & (plane != 7 - z)
-        four = (0, 1, 2, 3)
-
-        @pl.when(quad & plain)
+        plain = full & (d > 0)
+
+        @pl.when(valid & plain)
         def _():
-            absorb(which, chunk, 0, 4, four, off, skew, reach, False)
-
-        @pl.when(quad & jnp.logical_not(plain | lower | upper))
+            absorb(which, chunk, 0, 4, off, reach, False)
+
+        @pl.when(valid & jnp.logical_not(plain | lower | upper))
         def _():
-            absorb(which, chunk, 0, 4, four, off, skew, reach, True)
-
-        @pl.when(quad & (lower | upper))
+            absorb(which, chunk, 0, 4, off, reach, True)
+
+        @pl.when(valid & (lower | upper))
         def _():
             first = jnp.where(upper, 2, 0)
-            absorb(which, chunk, first, 2, four, off - first * 2 * ROWS, skew, reach, True)
-
-        start = jnp.where(own, 0, 1)
-
-        @pl.when(pair_only & plain)
-        def _():
-            absorb(which, chunk, 0, 4, (start, start + 2), off, skew, reach, False)
-
-        @pl.when(pair_only & jnp.logical_not(plain))
-        def _():
-            absorb(which, chunk, 0, 4, (start, start + 2), off, skew, reach, True)
+            absorb(which, chunk, first, 2, off - first * 2 * ROWS, reach, True)
 
         return 0
 
     def backs(which, t):
-        there = jnp.where(t % 2 == 1, 7 - z, z) * 8 if which == 2 else base
-        home = there + 2 * (2 * c + t // 2) + t % 2
+        home = base + 2 * (2 * c + t // 2) + t % 2
         i = 4 * which
         out = [Push(o.at[which, t], r.at[which, y], s_o.at[i + t], r_o.at[i + y], home, s, hd)]
         if which:
@@ -383,7 +376,7 @@
         lax.fori_loop(0, 4, one, 0)
 
     lax.fori_loop(0, len(TASKS), step, 0)
-    send_back(2)
+    send_back(1)
     for i in range(4):
         landed(r.at[0, i], r_o.at[i])
         merged[i] = r[0, i]
@@ -443,9 +436,10 @@
     project(hd)
     for one in sends:
         one.wait_send()
-    for h in range(7):
-        for j in range(2):
+    for j in range(2):
+        for h in range(6):
             full_down(h, j).wait_send()
+        full_up(j).wait_send()
     for h in range(8):
         when(needed(h), full_sib(h).wait_send)
     for kind in ("a", "b"):
@@ -469,7 +463,7 @@
 
 def whole(full_ids, spans, queries, keys_in, values_in, w):
     dma = pltpu.SemaphoreType.DMA
-    counts = (8, 8, 12, 12, 2, 2, 2, 2, 14, 14, 3, 3, 3, 3, 8, 8, 12, 12, 8, 8, 6, 6)
+    counts = (8, 8, 12, 12, 2, 2, 2, 2, 12, 12, 2, 2, 3, 3, 3, 3, 8, 8, 12, 12, 8, 8, 6, 6)
     smem = pl.BlockSpec(memory_space=pltpu.SMEM)
     return pl.pallas_call(
         whole_body,

time: 112 us -> 98.3 us (0.88)
  Pallas kernels: 108 us -> 94.7 us
    pallas_call x1, Pallas kernels: 108 us -> 94.7 us  [whole(): pl.pallas_call(whole_body, out_shape=jax.ShapeDtypeStruct((ROWS, 1024), B...]
where the time goes in v5:
time: 98.3 us; the launch traced here: 96.6 us
  Pallas kernels  94.7 us (96%)
  local copies, waits for them, and re-layouts  1.87 us (2%)
    pallas_call x1, Pallas kernels, whole(): pl.pallas_call(whole_body, out_shape=jax.ShapeDtypeStruct((ROWS, 1024), B...  94.7 us

profile of v5, /device:TPU:97, one launch (start us, length us, event | category | flops | bytes accessed | tf_op | source)
XLA Modules:
  0.0 96.6 jit_solution(2765070558629156294)
XLA Ops:
  0.0 94.7 %whole.1 = bf16[256,1024]{1,0:T(8,128)(2,1)} custom-call(s32[2]{0:T(128)} %ids.1, s32[8]{0:T(128)} %spans.1, bf16[256,1024]{1,0:T(8,128)(2,1)} %queries.1, bf16[256,1024]{1,0:T(8,128)(2,1)} %keys_in.1, bf16[256,1024]{1,0:T(8,128)(2,1)} %values_in.1, bf16[1024,4096]{1,0:T(8,128)(2,1)} %w.1), custom_call_target="tpu_custom_call" | custom-call | tf_op jit(solution)/shard_map/whole/pallas_call | solution.py:468
  94.7 1.9 %copy.8 = bf16[256,1024]{1,0:T(8,128)(2,1)} copy(bf16[256,1024]{1,0:T(8,128)(2,1)} %whole.1) | data formatting | bytes 1048576

commit v6 on v5

--- a/solution.py
+++ b/solution.py
@@ -75,22 +75,23 @@
     (0, 0, 1),
     (2, 0, 0),
     (2, 7, 0),
-    (1, 0, 0),
     (2, 1, 0),
     (0, 1, 0),
     (2, 2, 0),
     (0, 1, 1),
+    (1, 0, 0),
     (2, 3, 0),
-    (1, 1, 0),
     (2, 4, 0),
     (2, 5, 0),
     (0, 2, 0),
+    (0, 2, 1),
     (2, 6, 0),
-    (0, 2, 1),
+    (1, 1, 0),
     (1, 2, 0),
 )
-MOVES = {2: (("f", 7),), 3: (("b", 0),), 4: (("a", 1),), 8: (("b", 1),), 12: (("a", 2),), 15: (("b", 2),)}
-DONE = {15: 2, 16: 0}
+MOVES = {2: (("f", 7),), 4: (("a", 1),), 6: (("b", 0),), 11: (("b", 1),), 12: (("a", 2),), 16: (("b", 2),)}
+DONE = {14: 0, 15: 2}
+EARLY = 16
 
 
 def table(n, values):
@@ -102,16 +103,16 @@
 
 def whole_body(
     ids, spans, queries, keys_in, values_in, w, out,
-    qh, kvh, wv, kv, qb, o, lse, r, rl, merged, att, part, got, tmp, m_sc, l_sc, acc_sc, rel,
+    qh, kvh, wv, kv, qb, o, lse, r, rl, merged, att, part, got, tmp, ab, w_out, w_in, m_sc, l_sc, acc_sc, rel,
     w_sem, s_in, r_in, s_q, r_q, s_fa, r_fa, s_fb, r_fb, s_ff, r_ff, s_fu, r_fu, s_sa, r_sa, s_sb, r_sb, s_sf, r_sf,
-    s_o, r_o, s_l, r_l, s_x, r_x,
+    s_o, r_o, s_l, r_l, s_x, r_x, s_w, r_w, s_b, r_b,
 ):
     s, z, y, c, hd = position()
     pair, par = y // 2, y % 2
     base = z * 8
     up, down = (s + 8) % 64, (s + 56) % 64
     sib = base + 2 * y + (1 - c)
-    right, left = (hd + 1) % 4, (hd + 3) % 4
+    right, left, across = (hd + 1) % 4, (hd + 3) % 4, (hd + 2) % 4
     half = y // 2
     pltpu.make_async_copy(w, wv, w_sem).start()
     f0, f1 = ids[0] - hd * 8, ids[1] - hd * 8
@@ -134,7 +135,7 @@
             qh[i] = column_of(queries, i)
 
     arrange_kv((6, 7))
-    greet(plane_peers(s, hd) + [(up, hd), (down, hd), (s, right), (s, left)])
+    greet(plane_peers(s, hd) + [(up, hd), (down, hd), (s, right), (s, left), (s, across)])
 
     sends = []
 
@@ -243,6 +244,38 @@
     move_full(2, 0)
     push_q(1, lambda t: 4 + t // 2)
 
+    def round_head(src, dst, ssem, rsem):
+        return [
+            pltpu.make_async_remote_copy(
+                src_ref=src(group),
+                dst_ref=dst,
+                send_sem=ssem.at[i],
+                recv_sem=rsem.at[i],
+                device_id=(s, group),
+                device_id_type=MESH,
+            )
+            for i, group in enumerate((right, left, across))
+        ]
+
+    def arrived(ref, rsem):
+        for i, group in enumerate((left, right, across)):
+            landed(ref.at[group], rsem.at[i])
+
+    def weights_out():
+        return round_head(lambda group: w_out.at[group], w_in.at[hd], s_w, r_w)
+
+    def rows_out():
+        return round_head(lambda group: ab.at[hd], ab.at[hd], s_b, r_b)
+
+    landed(wv, w_sem)
+    for two in range(2):
+        h = jnp.clip(pick(jnp.int32(4 + two), f0, f1), 0, 7)
+        for group in range(4):
+            w_out[group, two * HD : (two + 1) * HD] = wv[h, :, group * 1024 : (group + 1) * 1024]
+    w_in[hd] = w_out[hd]
+    for copy in weights_out():
+        copy.start()
+
     reach_a = spans[jnp.clip(pick(y, f0, f1), 0, 7)]
     reach_b = spans[jnp.clip(pick(4 + pair, f0, f1), 0, 7)]
     q_start = base * ROWS + c * 4 * ROWS
@@ -290,6 +323,10 @@
             @pl.when(n == unit - 4)
             def _(unit=unit):
                 move_full(unit // 2, unit % 2)
+
+        @pl.when(n == EARLY)
+        def _():
+            sum_early()
 
         for at, moves in MOVES.items():
 
@@ -375,65 +412,82 @@
 
         lax.fori_loop(0, 4, one, 0)
 
-    lax.fori_loop(0, len(TASKS), step, 0)
-    send_back(1)
-    for i in range(4):
-        landed(r.at[0, i], r_o.at[i])
-        merged[i] = r[0, i]
-    for which in range(2):
+    def merge(which, two):
+        def column(i):
+            return jnp.tile(rl[which - 1, i], (16, 1)).T
+
+        first, second = 2 * two, 2 * two + 1
+        a, b = column(first), column(second)
+        top = jnp.maximum(a, b)
+        wa, wb = jnp.exp2(a - top), jnp.exp2(b - top)
+        value = wa * r[which, first].astype(F32) + wb * r[which, second].astype(F32)
+        return (value / (wa + wb)).astype(BF)
+
+    def rows_landed(which):
         for i in range(4):
-            landed(r.at[which + 1, i], r_o.at[4 * which + 4 + i])
-            landed(rl.at[which, i], r_l.at[4 * which + i])
-        for two in range(2):
-            first, second = 2 * two, 2 * two + 1
-
-            def column(i):
-                return jnp.tile(rl[which, i], (16, 1)).T
-
-            a, b = column(first), column(second)
-            top = jnp.maximum(a, b)
-            wa, wb = jnp.exp2(a - top), jnp.exp2(b - top)
-            value = wa * r[which + 1, first].astype(F32) + wb * r[which + 1, second].astype(F32)
-            merged[4 + 2 * which + two] = (value / (wa + wb)).astype(BF)
-    for h in range(8):
-        band = h - jnp.where(h > f0, 1, 0) - jnp.where(h > f1, 1, 0)
-        slot = jnp.where(f0 == h, 6, jnp.where(f1 == h, 7, jnp.clip(band, 0, 5)))
-        att[:, h * HD : (h + 1) * HD] = merged[slot]
-    landed(wv, w_sem)
+            landed(r.at[which, i], r_o.at[4 * which + i])
+            if which:
+                landed(rl.at[which - 1, i], r_l.at[4 * which - 4 + i])
 
     def project(dest):
         for side in range(2):
             for sub in range(2):
                 columns = pl.ds(pl.multiple_of(dest * 1024 + side * 512 + sub * 256, 256), 256)
-                piece = jnp.dot(att[...], wv[:, columns], preferred_element_type=F32)
+                piece = jnp.dot(att[...], wv[:, :, columns].reshape(1024, 256), preferred_element_type=F32)
                 part[dest, side, :, sub * 256 : (sub + 1) * 256] = piece.astype(BF)
 
-    def ship(src, slot, target):
-        one = pltpu.make_async_remote_copy(
-            src_ref=src,
+    def ship(slot):
+        src, target = (
+            (lambda: part.at[across, 0], right),
+            (lambda: part.at[across, 1], left),
+            (lambda: part.at[right, 1], right),
+            (lambda: part.at[left, 0], left),
+            (lambda: tmp.at[0], right),
+            (lambda: tmp.at[1], left),
+        )[slot]
+        return pltpu.make_async_remote_copy(
+            src_ref=src(),
             dst_ref=got.at[slot],
             send_sem=s_x.at[slot],
             recv_sem=r_x.at[slot],
             device_id=(s, target),
             device_id_type=MESH,
         )
-        one.start()
-        return one
-
-    across = (hd + 2) % 4
-    project(across)
-    moved = [ship(part.at[across, 0], 0, right), ship(part.at[across, 1], 1, left)]
-    project(right)
-    moved.append(ship(part.at[right, 1], 2, right))
-    project(left)
-    moved.append(ship(part.at[left, 0], 3, left))
+
+    def sum_early():
+        rows_landed(0)
+        for i in range(4):
+            merged[i] = r[0, i]
+        merged[4:6] = jnp.zeros((2, ROWS, HD), BF)
+        rows_landed(2)
+        for two in range(2):
+            merged[6 + two] = merge(2, two)
+        for h in range(8):
+            band = h - jnp.where(h > f0, 1, 0) - jnp.where(h > f1, 1, 0)
+            slot = jnp.where(f0 == h, 6, jnp.where(f1 == h, 7, jnp.clip(band, 0, 5)))
+            att[:, h * HD : (h + 1) * HD] = merged[slot]
+        project(across)
+        ship(0).start()
+        ship(1).start()
+        project(right)
+        ship(2).start()
+        project(left)
+        ship(3).start()
+
+    lax.fori_loop(0, len(TASKS), step, 0)
+    send_back(1)
     landed(got.at[0], r_x.at[0])
     tmp[0] = (got[0].astype(F32) + part[right, 0].astype(F32)).astype(BF)
-    moved.append(ship(tmp.at[0], 4, right))
+    ship(4).start()
     landed(got.at[1], r_x.at[1])
     tmp[1] = (got[1].astype(F32) + part[left, 1].astype(F32)).astype(BF)
-    moved.append(ship(tmp.at[1], 5, left))
+    ship(5).start()
     project(hd)
+    rows_landed(1)
+    for two in range(2):
+        ab[hd, :, two * HD : (two + 1) * HD] = merge(1, two)
+    for copy in rows_out():
+        copy.start()
     for one in sends:
         one.wait_send()
     for j in range(2):
@@ -451,19 +505,28 @@
         for t in range(4):
             for back in backs(which, t):
                 back.wait_send()
-    landed(got.at[2], r_x.at[2])
-    landed(got.at[3], r_x.at[3])
-    landed(got.at[4], r_x.at[4])
-    out[:, :512] = (part[hd, 0].astype(F32) + got[4].astype(F32) + got[3].astype(F32)).astype(BF)
-    landed(got.at[5], r_x.at[5])
-    out[:, 512:] = (part[hd, 1].astype(F32) + got[5].astype(F32) + got[2].astype(F32)).astype(BF)
-    for one in moved:
-        one.wait_send()
+    for copy in weights_out():
+        copy.wait_send()
+    arrived(w_in, r_w)
+    for i in range(2, 6):
+        landed(got.at[i], r_x.at[i])
+    arrived(ab, r_b)
+    for side in range(2):
+        total = part[hd, side].astype(F32) + got[4 + side].astype(F32) + got[3 - side].astype(F32)
+        for group in range(4):
+            total = total + jnp.dot(
+                ab[group], w_in[group, :, side * 512 : (side + 1) * 512], preferred_element_type=F32
+            )
+        out[:, side * 512 : (side + 1) * 512] = total.astype(BF)
+    for copy in rows_out():
+        copy.wait_send()
+    for i in range(6):
+        ship(i).wait_send()
 
 
 def whole(full_ids, spans, queries, keys_in, values_in, w):
     dma = pltpu.SemaphoreType.DMA
-    counts = (8, 8, 12, 12, 2, 2, 2, 2, 12, 12, 2, 2, 3, 3, 3, 3, 8, 8, 12, 12, 8, 8, 6, 6)
+    counts = (8, 8, 12, 12, 2, 2, 2, 2, 12, 12, 2, 2, 3, 3, 3, 3, 8, 8, 12, 12, 8, 8, 6, 6, 3, 3, 3, 3)
     smem = pl.BlockSpec(memory_space=pltpu.SMEM)
     return pl.pallas_call(
         whole_body,
@@ -473,7 +536,7 @@
         scratch_shapes=[
             pltpu.VMEM((8, ROWS, HD), BF),
             pltpu.VMEM((8, 2, ROWS, HD), BF),
-            pltpu.VMEM((1024, 4096), BF),
+            pltpu.VMEM((8, HD, 4096), BF),
             pltpu.VMEM((17, 4, 2, ROWS, HD), BF),
             pltpu.VMEM((3, 4, ROWS, HD), BF),
             pltpu.VMEM((3, 4, ROWS, HD), BF),
@@ -485,6 +548,9 @@
             pltpu.VMEM((4, 2, ROWS, 512), BF),
             pltpu.VMEM((6, ROWS, 512), BF),
             pltpu.VMEM((2, ROWS, 512), BF),
+            pltpu.VMEM((4, ROWS, 2 * HD), BF),
+            pltpu.VMEM((4, 2 * HD, 1024), BF),
+            pltpu.VMEM((4, 2 * HD, 1024), BF),
             pltpu.VMEM((3, 4, ROWS, HD), F32),
             pltpu.VMEM((3, 4, ROWS, HD), F32),
             pltpu.VMEM((3, 4, ROWS, HD), F32),
@@ -498,7 +564,7 @@
 
 
 def on_device(queries, keys_in, values_in, out_weight, spans, full_ids):
-    return whole(full_ids, spans, queries, keys_in, values_in, out_weight)
+    return whole(full_ids, spans, queries, keys_in, values_in, out_weight.reshape(8, HD, 4096))
 
 
 def solution(mesh):

time: 98.3 us -> 102 us (1.038)
  Pallas kernels: 94.7 us -> 98 us
    pallas_call x1, Pallas kernels: 94.7 us -> 98 us  [whole(): pl.pallas_call(whole_body, out_shape=jax.ShapeDtypeStruct((ROWS, 1024), B...]
where the time goes in v6:
time: 102 us; the launch traced here: 99.9 us
  Pallas kernels  98 us (96%)
  local copies, waits for them, and re-layouts  1.87 us (2%)
    pallas_call x1, Pallas kernels, whole(): pl.pallas_call(whole_body, out_shape=jax.ShapeDtypeStruct((ROWS, 1024), B...  98 us

profile of v6, /device:TPU:97, one launch (start us, length us, event | category | flops | bytes accessed | tf_op | source)
XLA Modules:
  0.0 99.9 jit_solution(15943537765433970723)
XLA Ops:
  0.0 98.0 %whole.1 = bf16[256,1024]{1,0:T(8,128)(2,1)} custom-call(s32[2]{0:T(128)} %ids.1, s32[8]{0:T(128)} %spans.1, bf16[256,1024]{1,0:T(8,128)(2,1)} %queries.1, bf16[256,1024]{1,0:T(8,128)(2,1)} %keys_in.1, bf16[256,1024]{1,0:T(8,128)(2,1)} %values_in.1, bf16[8,128,4096]{2,1,0:T(8,128)(2,1)} %bitcast.1), custom_call_target="tpu_custom_call" | custom-call | tf_op jit(solution)/shard_map/whole/pallas_call | solution.py:531
  98.0 1.9 %copy.8 = bf16[256,1024]{1,0:T(8,128)(2,1)} copy(bf16[256,1024]{1,0:T(8,128)(2,1)} %whole.1) | data formatting | bytes 1048576

commit v7 on v5

--- a/solution.py
+++ b/solution.py
@@ -259,7 +259,10 @@
             if masked:
                 at = rel[:, :keys]
                 low = -(off + t * ROWS)
-                sc = jnp.where((at >= low) & (at < low + reach), sc, FILL)
+                seen = at < low + reach
+                if masked == 2:
+                    seen = seen & (at >= low)
+                sc = jnp.where(seen, sc, FILL)
             return sc
 
         def soft(t, sc):
@@ -339,16 +342,20 @@
 
         @pl.when(valid & plain)
         def _():
-            absorb(which, chunk, 0, 4, off, reach, False)
-
-        @pl.when(valid & jnp.logical_not(plain | lower | upper))
-        def _():
-            absorb(which, chunk, 0, 4, off, reach, True)
+            absorb(which, chunk, 0, 4, off, reach, 0)
+
+        @pl.when(valid & (d == 0) & jnp.logical_not(lower))
+        def _():
+            absorb(which, chunk, 0, 4, off, reach, 2)
+
+        @pl.when(valid & (d > 0) & jnp.logical_not(plain | upper))
+        def _():
+            absorb(which, chunk, 0, 4, off, reach, 1)
 
         @pl.when(valid & (lower | upper))
         def _():
             first = jnp.where(upper, 2, 0)
-            absorb(which, chunk, first, 2, off - first * 2 * ROWS, reach, True)
+            absorb(which, chunk, first, 2, off - first * 2 * ROWS, reach, 2)
 
         return 0
 
@@ -380,7 +387,7 @@
     for i in range(4):
         landed(r.at[0, i], r_o.at[i])
         merged[i] = r[0, i]
-    for which in range(2):
+    for which in (1, 0):
         for i in range(4):
             landed(r.at[which + 1, i], r_o.at[4 * which + 4 + i])
             landed(rl.at[which, i], r_l.at[4 * which + i])
@@ -401,8 +408,8 @@
         att[:, h * HD : (h + 1) * HD] = merged[slot]
     landed(wv, w_sem)
 
-    def project(dest):
-        for side in range(2):
+    def project(dest, sides=(0, 1)):
+        for side in sides:
             for sub in range(2):
                 columns = pl.ds(pl.multiple_of(dest * 1024 + side * 512 + sub * 256, 256), 256)
                 piece = jnp.dot(att[...], wv[:, columns], preferred_element_type=F32)
@@ -421,8 +428,10 @@
         return one
 
     across = (hd + 2) % 4
-    project(across)
-    moved = [ship(part.at[across, 0], 0, right), ship(part.at[across, 1], 1, left)]
+    project(across, (0,))
+    moved = [ship(part.at[across, 0], 0, right)]
+    project(across, (1,))
+    moved.append(ship(part.at[across, 1], 1, left))
     project(right)
     moved.append(ship(part.at[right, 1], 2, right))
     project(left)

time: 98.3 us -> 96.9 us (0.986)
  the two profiles are of different devices: /device:TPU:97 before, /device:TPU:193 now
where the time goes in v7:
time: 96.9 us; the launch traced here: 96.8 us
  Pallas kernels  94.9 us (98%)
  local copies, waits for them, and re-layouts  1.87 us (2%)
    pallas_call x1, Pallas kernels, whole(): pl.pallas_call(whole_body, out_shape=jax.ShapeDtypeStruct((ROWS, 1024), B...  94.9 us

profile of v7, /device:TPU:193, one launch (start us, length us, event | category | flops | bytes accessed | tf_op | source)
XLA Modules:
  0.0 96.8 jit_solution(4502171476399897737)
XLA Ops:
  0.0 94.9 %whole.1 = bf16[256,1024]{1,0:T(8,128)(2,1)} custom-call(s32[2]{0:T(128)} %ids.1, s32[8]{0:T(128)} %spans.1, bf16[256,1024]{1,0:T(8,128)(2,1)} %queries.1, bf16[256,1024]{1,0:T(8,128)(2,1)} %keys_in.1, bf16[256,1024]{1,0:T(8,128)(2,1)} %values_in.1, bf16[1024,4096]{1,0:T(8,128)(2,1)} %w.1), custom_call_target="tpu_custom_call" | custom-call | tf_op jit(solution)/shard_map/whole/pallas_call | solution.py:477
  94.9 1.9 %copy.8 = bf16[256,1024]{1,0:T(8,128)(2,1)} copy(bf16[256,1024]{1,0:T(8,128)(2,1)} %whole.1) | data formatting | bytes 1048576
